TPU v7x, 512 devices: a whole 4x8x8 slice. The times are simulated.
512 devices in a mesh: imp: 32 (over z, x), adv: 16 (over y, core).
Axes of the slice: x: 4, y: 8, z: 8, core: 2. Of those that a mesh axis runs over, the one named last changes fastest.
Arguments:
- impression_vectors: bfloat16 [64, 65536], P(None, 'imp'), may hold values from -6 to 6
- advertiser_vectors: bfloat16 [64, 65536], P(None, ('imp', 'adv')), may hold values from -0.75 to 0.75
- spend_limits: float32 [65536], P(('imp', 'adv')), may hold values from 1024 to 8192
- capacity: float32 [65536], P('imp'), may hold values from 1024 to 8192
- blocks: int32 [512, 16, 8], P('imp', 'adv'), may hold values from 0 to 511, as said below
- counts: int32 [512, 16], P('imp', 'adv'), may hold values from 1 to 8, as said below
Outputs:
- prices: float32 [65536], P(('imp', 'adv'))
- impression_duals: float32 [65536], P('imp')
- impression_grad: bfloat16 [64, 65536], P(None, ('imp', 'adv'))
- advertiser_grad: bfloat16 [64, 65536], P(None, ('imp', 'adv'))
Inputs may be any that keep to these rules, and one draw needn't show every extreme that they name: Block numbers. Entry [g, a, k] names a block b with (b) % (the size of adv) == a. The 8 entries of one list are distinct; entries at slots k >= counts[g, a] are padding and name valid blocks too. `counts`: every group has one index of adv whose count is 8.
All inputs are finite; a program needn't handle non-finite values.
Results may differ from a plain program's by a relative error of at most 0.012.
Values may be sent and summed in bfloat16 or wider, within the bound.
No kernel may reach another device: no remote copies, remote signals or barrier semaphores. Data moves between devices by JAX's collectives and lax.ppermute only.
A program may use at most 64 MiB of HBM per device.

v0:
```python
import jax
import jax.numpy as jnp
from jax import lax
from jax.sharding import PartitionSpec as P

GROUP = 128
BLOCK = 128
ITERS = 3
BLK_DEV = 1


def local(impression_vectors, advertiser_vectors, spend_limits, capacity, blocks, counts):
    features = impression_vectors.shape[0]
    groups_here = blocks.shape[0]
    slot_count = blocks.shape[2]
    adv_devices = lax.axis_size("adv")
    block_ids = blocks.reshape(groups_here, slot_count)
    local_ids = block_ids // BLK_DEV // adv_devices * BLK_DEV + block_ids % BLK_DEV
    live_slots = (jnp.arange(slot_count)[None, :] < counts).astype(jnp.float32)
    viewers = impression_vectors.reshape(features, groups_here, GROUP)
    extent = slot_count * BLOCK
    own_count = spend_limits.shape[0]
    fetched = lax.all_gather(advertiser_vectors, "imp", axis=1, tiled=True)
    catalog = fetched.reshape(features, fetched.shape[1] // BLOCK, BLOCK)
    local_blocks = catalog.shape[1]

    def allocate(source, prices, duals, group_no):
        chosen = lax.dynamic_index_in_dim(local_ids, group_no, 0, keepdims=False)
        columns = jnp.take(source, chosen, axis=1).reshape(features, extent)
        viewer = lax.dynamic_index_in_dim(viewers, group_no, 1, keepdims=False)
        scores = lax.dot_general(
            viewer, columns, (((0,), (0,)), ((), ())), preferred_element_type=jnp.float32
        )
        charged = jnp.take(prices, chosen, axis=0).reshape(extent)
        shadow = lax.dynamic_slice_in_dim(duals, group_no * GROUP, GROUP)
        eligible = jnp.repeat(
            lax.dynamic_index_in_dim(live_slots, group_no, 0, keepdims=False), BLOCK
        )
        shares = jnp.clip(scores - charged[None, :] - shadow[:, None], 0.0, 1.0) * eligible[None, :]
        return (shares, chosen, columns, viewer)

    duals = jnp.zeros((groups_here * GROUP,), jnp.float32)
    range_prices = jnp.zeros((local_blocks, BLOCK), jnp.float32)
    own_prices = jnp.zeros((own_count,), jnp.float32)
    for iteration in range(ITERS):
        totals_prices = range_prices

        def advance(group_no, pair):
            outlay, demand = pair
            shares, chosen, _, _ = allocate(catalog, totals_prices, duals, group_no)
            outlay = outlay.at[chosen].add(jnp.sum(shares, axis=0).reshape(slot_count, BLOCK))
            demand = lax.dynamic_update_slice_in_dim(
                demand, jnp.sum(shares, axis=1), group_no * GROUP, 0
            )
            return (outlay, demand)

        totals_start = (
            jnp.zeros((local_blocks, BLOCK), jnp.float32),
            jnp.zeros((groups_here * GROUP,), jnp.float32),
        )
        outlay, demand = lax.fori_loop(0, groups_here, advance, totals_start)
        own_outlay = lax.psum_scatter(outlay.reshape(-1), "imp", scatter_dimension=0, tiled=True)
        dual_demand = demand
        dual_demand = lax.psum(dual_demand, "adv")
        duals = jnp.maximum(duals + dual_demand / capacity - 1.0, 0.0)
        own_prices = jnp.maximum(own_prices + own_outlay / spend_limits - 1.0, 0.0)
        range_prices = lax.all_gather(own_prices, "imp", axis=0, tiled=True).reshape(
            local_blocks, BLOCK
        )

    def grad_step(group_no, pair):
        imp_part, adv_part = pair
        shares, chosen, columns, viewer = allocate(catalog, range_prices, duals, group_no)
        weights = shares.astype(jnp.bfloat16)
        imp_cols = lax.dot_general(
            columns, weights, (((1,), (1,)), ((), ())), preferred_element_type=jnp.float32
        )
        imp_part = lax.dynamic_update_slice_in_dim(imp_part, imp_cols, group_no * GROUP, 1)
        adv_terms = jnp.dot(viewer, weights, preferred_element_type=jnp.float32).reshape(
            features, slot_count, BLOCK
        )
        adv_part = adv_part.at[:, chosen].add(adv_terms)
        return (imp_part, adv_part)

    start = (
        jnp.zeros((features, groups_here * GROUP), jnp.float32),
        jnp.zeros((features, local_blocks, BLOCK), jnp.float32),
    )
    imp_part, adv_part = lax.fori_loop(0, groups_here, grad_step, start)
    impression_grad = lax.psum_scatter(imp_part, "adv", scatter_dimension=1, tiled=True).astype(
        jnp.bfloat16
    )
    adv_rounded = (adv_part.reshape(features, -1) / GROUP).astype(jnp.bfloat16)
    advertiser_grad = (
        lax.psum_scatter(adv_rounded, "imp", scatter_dimension=1, tiled=True)
        .astype(jnp.float32)
        .astype(jnp.bfloat16)
    )
    return (own_prices, duals, impression_grad, advertiser_grad)


def solution(mesh):
    return jax.shard_map(
        local,
        mesh=mesh,
        in_specs=(
            P(None, "imp"),
            P(None, ("imp", "adv")),
            P(("imp", "adv")),
            P("imp"),
            P("imp", "adv", None),
            P("imp", "adv"),
        ),
        out_specs=(P(("imp", "adv")), P("imp"), P(None, ("imp", "adv")), P(None, ("imp", "adv"))),
        check_vma=False,
    )
```

profile of v0, /device:TPU:29, one launch (start us, length us, event | category | flops | bytes accessed | tf_op | source)
XLA Modules:
  0.0 1180.3 jit_solution(11911110707107156288)
XLA Ops:
  7.2 0.7 copy-done.12
  8.0 0.7 copy-done.14
  8.8 0.6 copy-done.7
  9.5 44.3 %all_gather.12 = bf16[64,4096]{1,0:T(8,128)(2,1)S(1)} all-gather(bf16[64,128]{1,0:T(8,128)(2,1)S(1)} %copy-done.7), channel_id=1, replica_groups=mesh['imp'=32,'adv'=16] {'imp'}, dimensions={1}, use_global_device_ids=true | all-gather | bytes 540672 | tf_op jit(solution)/shard_map/all_gather | solution.py:23
  53.9 41.5 %while.60 = (s32[]{:T(128)}, f32[32,128]{1,0:T(8,128)S(1)}, f32[2048]{0:T(1024)S(1)}, s32[16,8]{1,0:T(8,128)S(1)}, bf16[64,16,128]{2,0,1:T(8,128)(2,1)S(1)}, /*i...) while((s32[]{:T(128)}, f32[32,128]{1,0:T(8,128)S(1)}, ...), condition=%wide.region_4.7_spmd, body=%wide.region_0.6_spmd.sunk | while | flops 17500104 | bytes 485907 | solution.py:61
  55.9 0.6 scatter_custom_fusion.15
  58.5 0.6 scatter_custom_fusion.15
  61.1 0.6 scatter_custom_fusion.15
  68.9 0.6 scatter_custom_fusion.15
  84.5 0.6 scatter_custom_fusion.15
  95.5 35.5 %psum.21 = f32[2048]{0:T(1024)S(1)} all-reduce(f32[2048]{0:T(1024)S(1)} %get-tuple-element.597), channel_id=1, replica_groups=mesh['imp'=32,'adv'=16] {'adv'}, use_global_device_ids=true, to_apply=%region_6.9 | all-reduce | flops 2048 | bytes 16384 | tf_op jit(solution)/shard_map/psum | solution.py:64
  131.0 108.5 %all-reduce = f32[4096]{0:T(1024)S(1)} all-reduce(f32[4096]{0:T(1024)S(1)} %bitcast.255), channel_id=2, replica_groups=mesh['imp'=32,'adv'=16] {'imp'}, use_global_device_ids=true, to_apply=%region_5.8.clone | all-reduce | flops 4096 | bytes 32768
  239.5 1.3 dynamic-slice
  241.5 30.3 %all-gather = f32[32,1,128]{2,1,0:T(1,128)S(1)} all-gather(f32[1,1,128]{2,1,0:T(1,128)S(1)} %bitcast.260), channel_id=1, replica_groups=mesh['imp'=32,'adv'=16] {'imp'}, dimensions={0}, use_global_device_ids=true | all-gather | bytes 16896 | tf_op jit(solution)/shard_map/all_gather | solution.py:67
  271.9 42.5 %while.61 = (s32[]{:T(128)}, f32[32,128]{1,0:T(8,128)S(1)}, f32[2048]{0:T(1024)S(1)}, s32[16,8]{1,0:T(8,128)S(1)}, bf16[64,16,128]{2,0,1:T(8,128)(2,1)S(1)}, /*i...) while((s32[]{:T(128)}, f32[32,128]{1,0:T(8,128)S(1)}, ...), condition=%wide.region_11.14_spmd, body=%wide.region_7.13_spmd.sunk | while | flops 17631180 | bytes 471067 | solution.py:61
  276.6 0.6 scatter_custom_fusion.17
  284.6 0.6 scatter_custom_fusion.17
  314.3 59.8 %psum.22 = f32[2048]{0:T(1024)S(1)} all-reduce(f32[2048]{0:T(1024)S(1)} %get-tuple-element.599), channel_id=1, replica_groups=mesh['imp'=32,'adv'=16] {'adv'}, use_global_device_ids=true, to_apply=%region_13.16 | all-reduce | flops 2048 | bytes 16384 | tf_op jit(solution)/shard_map/psum | solution.py:64
  374.2 108.6 %all-reduce.1 = f32[4096]{0:T(1024)S(1)} all-reduce(f32[4096]{0:T(1024)S(1)} %bitcast.256), channel_id=3, replica_groups=mesh['imp'=32,'adv'=16] {'imp'}, use_global_device_ids=true, to_apply=%region_12.15.clone | all-reduce | flops 4096 | bytes 32768
  482.9 29.9 %all-gather.1 = f32[32,1,128]{2,1,0:T(1,128)S(1)} all-gather(f32[1,1,128]{2,1,0:T(1,128)S(1)} %bitcast.259), channel_id=1, replica_groups=mesh['imp'=32,'adv'=16] {'imp'}, dimensions={0}, use_global_device_ids=true | all-gather | bytes 16896 | tf_op jit(solution)/shard_map/all_gather | solution.py:67
  512.8 42.5 %while.62 = (s32[]{:T(128)}, f32[32,128]{1,0:T(8,128)S(1)}, f32[2048]{0:T(1024)S(1)}, s32[16,8]{1,0:T(8,128)S(1)}, bf16[64,16,128]{2,0,1:T(8,128)(2,1)S(1)}, /*i...) while((s32[]{:T(128)}, f32[32,128]{1,0:T(8,128)S(1)}, ...), condition=%wide.region_18.21_spmd, body=%wide.region_14.20_spmd.sunk | while | flops 17631180 | bytes 471067 | solution.py:61
  555.3 60.5 %psum.23 = f32[2048]{0:T(1024)S(1)} all-reduce(f32[2048]{0:T(1024)S(1)} %get-tuple-element.601), channel_id=1, replica_groups=mesh['imp'=32,'adv'=16] {'adv'}, use_global_device_ids=true, to_apply=%region_20.23 | all-reduce | flops 2048 | bytes 16384 | tf_op jit(solution)/shard_map/psum | solution.py:64
  616.4 108.3 %all-reduce.2 = f32[4096]{0:T(1024)S(1)} all-reduce(f32[4096]{0:T(1024)S(1)} %bitcast.257), channel_id=4, replica_groups=mesh['imp'=32,'adv'=16] {'imp'}, use_global_device_ids=true, to_apply=%region_19.22.clone | all-reduce | flops 4096 | bytes 32768
  725.3 30.2 %all-gather.2 = f32[32,1,128]{2,1,0:T(1,128)S(1)} all-gather(f32[1,1,128]{2,1,0:T(1,128)S(1)} %bitcast.261), channel_id=1, replica_groups=mesh['imp'=32,'adv'=16] {'imp'}, dimensions={0}, use_global_device_ids=true | all-gather | bytes 16896 | tf_op jit(solution)/shard_map/all_gather | solution.py:67
  755.6 95.1 %while.63 = (s32[]{:T(128)}, f32[64,2048]{1,0:T(8,128)S(1)}, f32[64,32,128]{2,0,1:T(8,128)S(1)}, s32[16,8]{1,0:T(8,128)S(1)}, bf16[64,32,128]{2,0,1:T(8,128)(2,1...) while((s32[]{:T(128)}, f32[64,2048]{1,0:T(8,128)S(1)}, ...), condition=%wide.region_23.26_spmd, body=%wide.region_21.25_spmd.sunk | while | flops 51185740 | bytes 2993603 | solution.py:89
  756.2 0.8 dynamic_slice.201
  760.6 0.9 scatter_fusion
  762.2 0.8 dynamic_slice.201
  766.6 0.9 scatter_fusion
  768.1 0.8 dynamic_slice.201
  772.5 0.9 scatter_fusion
  774.1 0.8 dynamic_slice.201
  778.5 0.9 scatter_fusion
  780.0 0.8 dynamic_slice.201
  784.4 0.9 scatter_fusion
  786.0 0.8 dynamic_slice.201
  790.4 0.9 scatter_fusion
  791.9 0.8 dynamic_slice.201
  796.3 0.9 scatter_fusion
  797.9 0.8 dynamic_slice.201
  802.3 0.9 scatter_fusion
  803.8 0.8 dynamic_slice.201
  808.2 0.9 scatter_fusion
  809.7 0.8 dynamic_slice.201
  814.2 0.9 scatter_fusion
  815.7 0.8 dynamic_slice.201
  820.1 0.9 scatter_fusion
  821.6 0.8 dynamic_slice.201
  826.0 0.9 scatter_fusion
  827.6 0.8 dynamic_slice.201
  832.0 0.9 scatter_fusion
  833.5 0.8 dynamic_slice.201
  837.9 0.9 scatter_fusion
  839.5 0.8 dynamic_slice.201
  843.9 0.9 scatter_fusion
  845.4 0.8 dynamic_slice.201
  849.8 0.9 scatter_fusion
  850.9 0.7 copy-done.1
  851.6 1.3 copy.68
  853.0 0.7 reduce-scatter.5.cloned.1.call-update
  853.7 251.4 %reduce-scatter.7.cloned.1.call-done = bf16[128,64]{1,0:T(8,128)(2,1)} async-done(((bf16[4096,64]{1,0:T(8,128)(2,1)}), bf16[128,64]{1,0:T(8,128)(2,1)}) %reduce-scatter.7.cloned.1.call-update) | async-done | bytes 16400
  1105.0 1.4 copy.67
  1106.5 65.6 %reduce-scatter.5.cloned.1.call-done = f32[64,128]{1,0:T(8,128)} async-done(((f32[64,2048]{1,0:T(8,128)}), f32[64,128]{1,0:T(8,128)}) %reduce-scatter.5.cloned.1.call-update) | async-done | bytes 32784 | tf_op jit(solution)/shard_map/reduce_scatter | solution.py:90
  1172.1 1.4 convert_element_type.23
  (956 shorter events, 187.8 us)
Async XLA Ops:
  7.2 1.6 copy-start
  7.2 1097.9 %reduce-scatter.7.cloned.1.call-start = ((), (), s32[]{:S(2)}) async-start(), calls=%async_computation.3 | async-start | bytes 1081344
  241.5 30.3 %copy-start.2 = (f32[2048]{0:T(1024)S(1)}, f32[2048]{0:T(1024)}, u32[]{:S(2)}) copy-start(f32[2048]{0:T(1024)} %param.21) | copy-start | bytes 24580
  755.6 2.0 copy-start.5
  757.6 1.2 copy-start.3
  760.6 0.9 copy-start.6
  760.6 0.9 copy-start.10
  761.6 2.0 copy-start.5
  763.6 1.2 copy-start.3
  766.6 0.9 copy-start.6
  766.6 0.9 copy-start.10
  767.5 2.0 copy-start.5
  769.5 1.2 copy-start.3
  772.5 0.9 copy-start.6
  772.5 0.9 copy-start.10
  773.5 2.0 copy-start.5
  775.4 1.2 copy-start.3
  778.5 0.9 copy-start.6
  778.5 0.9 copy-start.10
  779.4 2.0 copy-start.5
  781.4 1.2 copy-start.3
  784.4 0.9 copy-start.6
  784.4 0.9 copy-start.10
  785.4 2.0 copy-start.5
  787.3 1.2 copy-start.3
  790.4 0.9 copy-start.6
  790.4 0.9 copy-start.10
  791.3 2.0 copy-start.5
  793.3 1.2 copy-start.3
  796.3 0.9 copy-start.6
  796.3 0.9 copy-start.10
  797.3 2.0 copy-start.5
  799.2 1.2 copy-start.3
  802.3 0.9 copy-start.6
  802.3 0.9 copy-start.10
  803.2 2.0 copy-start.5
  805.2 1.2 copy-start.3
  808.2 0.9 copy-start.6
  808.2 0.9 copy-start.10
  809.1 2.0 copy-start.5
  811.1 1.2 copy-start.3
  814.2 0.9 copy-start.6
  814.2 0.9 copy-start.10
  815.1 2.0 copy-start.5
  817.1 1.2 copy-start.3
  820.1 0.9 copy-start.6
  820.1 0.9 copy-start.10
  821.0 2.0 copy-start.5
  823.0 1.2 copy-start.3
  826.0 0.9 copy-start.10
  827.0 2.0 copy-start.5
  829.0 1.2 copy-start.3
  832.0 0.9 copy-start.10
  832.9 2.0 copy-start.5
  834.9 1.2 copy-start.3
  837.9 0.9 copy-start.6
  837.9 0.9 copy-start.10
  838.9 2.0 copy-start.5
  840.8 1.2 copy-start.3
  843.9 0.9 copy-start.10
  844.8 2.0 copy-start.5
  846.8 1.2 copy-start.3
  849.8 0.9 copy-start.10
  852.9 319.1 %reduce-scatter.5.cloned.1.call-start = ((), (), s32[]{:S(2)}) async-start(), calls=%async_computation.2 | async-start | bytes 557056 | tf_op jit(solution)/shard_map/reduce_scatter | solution.py:90
  (58 other events, 38.3 us)
Sparse Core Ops, SparseCore 0:
  853.1 251.9 reduce-scatter.6
  1107.8 64.1 reduce-scatter.4
where the time goes:
time: 1180 us
  blocking collectives  616 us (52%)
  waiting for transfers between devices  318 us (27%)
  local copies, waits for them, and re-layouts  133 us (11%)
  other arithmetic  62.3 us (5%)
  matrix products  30.7 us (3%)
  between operations  14.9 us (1%)
    unnamed x3, blocking collectives  325 us
    unnamed x3, waiting for transfers between devices  252 us
    psum x3, blocking collectives, local(): dual_demand = lax.psum(dual_demand, 'adv')  156 us
    all_gather x3, blocking collectives, local(): lax.all_gather(own_prices, 'imp', axis=0, tiled=True)  90.4 us
    reduce_scatter x1, waiting for transfers between devices, local(): lax.psum_scatter(imp_part, 'adv', scatter_dimension=1, tiled=True)  65.6 us
    all_gather x1, blocking collectives, local(): fetched = lax.all_gather(advertiser_vectors, 'imp', axis=1, tiled=True)  44.3 us
    gather x64, local copies, waits for them, and re-layouts, allocate(): columns = jnp.take(source, chosen, axis=1).reshape(features, extent)  36.6 us
    gather x64, local copies, waits for them, and re-layouts, allocate(): charged = jnp.take(prices, chosen, axis=0).reshape(extent)  35.6 us
  transfers between devices with their start and end apart: 2, of which 2 were waited for; matrix products, arithmetic and copies ran while one was open for 0% of the time, Pallas kernels for 0%

commit v1 on v0

v1 whole, which is shorter than its diff:
```python
import functools

import jax
import jax.numpy as jnp
from jax import lax
from jax.experimental import pallas as pl
from jax.experimental.pallas import tpu as pltpu
from jax.sharding import PartitionSpec as P


GROUP = 128
BLOCK = 128
PENALTY = 1e30

VMEM = pl.BlockSpec(memory_space=pltpu.VMEM)
SMEM = pl.BlockSpec(memory_space=pltpu.SMEM)
F32 = jnp.float32
BF16 = jnp.bfloat16
IMP = ("z", "x")
ADV = ("y", "core")
PARAMS = pltpu.CompilerParams(vmem_limit_bytes=16 << 20)


def slot_shares(group_no, slot, ids, counts, catalog, viewer, prices, shadow):
    first, second = ids[group_no, slot], ids[group_no, slot + 1]
    columns = jnp.concatenate([catalog[first], catalog[second]], axis=1)
    scores = jnp.dot(viewer, columns, preferred_element_type=F32)
    count = counts[group_no, 0]
    rows = []
    for place, block in ((slot, first), (slot + 1, second)):
        dead = jnp.where(place < count, 0.0, PENALTY).astype(F32)
        charged = dead if prices is None else prices[pl.ds(block, 1), :] + dead
        rows.append(jnp.broadcast_to(charged, (1, BLOCK)))
    scores = scores - jnp.concatenate(rows, axis=1)
    if shadow is not None:
        scores = scores - jnp.concatenate([shadow, shadow], axis=1)
    return jnp.clip(scores, 0.0, 1.0), columns, first, second


def column(row):
    return jnp.broadcast_to(row, (row.shape[1], row.shape[1])).T


def totals_kernel(first_pass, ids, counts, catalog, viewers_t, *refs):
    groups, slots = ids.shape
    if first_pass:
        outlay_out, demand_out, outlay_acc = refs
        prices = duals = None
    else:
        (outlays, old_prices, rate, duals,
         outlay_out, demand_out, prices, outlay_acc) = refs
        prices[...] = jnp.maximum(
            old_prices[...] + jnp.sum(outlays[...], axis=0) * rate[...] - 1.0, 0.0
        )
    outlay_acc[...] = jnp.zeros_like(outlay_acc)

    def step(group_no, _):
        start = pl.multiple_of(group_no * GROUP, GROUP)
        viewer = viewers_t[pl.ds(start, GROUP), :]
        shadow = None if first_pass else column(duals[pl.ds(group_no, 1), :])
        by_viewer = jnp.zeros((GROUP, BLOCK), F32)
        for slot in range(0, slots, 2):
            shares, _, first, second = slot_shares(
                group_no, slot, ids, counts, catalog, viewer, prices, shadow
            )
            by_viewer = by_viewer + (shares[:, :BLOCK] + shares[:, BLOCK:])
            folded = jnp.sum(shares.reshape(GROUP // 8, 8, 2 * BLOCK), axis=0)
            outlay_acc[first] += folded[:, :BLOCK]
            outlay_acc[second] += folded[:, BLOCK:]
        demand_out[pl.ds(group_no, 1), :] = jnp.sum(by_viewer.T, axis=0, keepdims=True)
        return 0

    lax.fori_loop(0, groups, step, 0)
    outlay = jnp.sum(outlay_acc[...], axis=1)
    for peer in range(outlay_out.shape[0]):
        outlay_out[peer] = outlay


def grads_kernel(
    ids, counts, catalog, viewers_t, viewers, outlays, old_prices, rate, duals,
    imp_out, adv_out, prices, adv_acc,
):
    groups, slots = ids.shape
    features = viewers.shape[0]
    prices[...] = jnp.maximum(
        old_prices[...] + jnp.sum(outlays[...], axis=0) * rate[...] - 1.0, 0.0
    )
    adv_acc[...] = jnp.zeros_like(adv_acc)

    def step(group_no, _):
        start = pl.multiple_of(group_no * GROUP, GROUP)
        viewer_t = viewers_t[pl.ds(start, GROUP), :]
        viewer = viewers[:, pl.ds(start, GROUP)]
        shadow = column(duals[pl.ds(group_no, 1), :])
        imp_part = jnp.zeros((features, GROUP), F32)
        for slot in range(0, slots, 2):
            shares, columns, first, second = slot_shares(
                group_no, slot, ids, counts, catalog, viewer_t, prices, shadow
            )
            weights = shares.astype(BF16)
            imp_part = imp_part + lax.dot_general(
                columns, weights, (((1,), (1,)), ((), ())), preferred_element_type=F32
            )
            adv_terms = jnp.dot(viewer, weights, preferred_element_type=F32)
            adv_acc[first] += adv_terms[:, :BLOCK]
            adv_acc[second] += adv_terms[:, BLOCK:]
        imp_out[group_no] = imp_part.astype(BF16)
        return 0

    lax.fori_loop(0, groups, step, 0)
    adv_out[...] = (adv_acc[...] * (1.0 / GROUP)).astype(BF16)


def spread(value, axis):
    copies = jnp.broadcast_to(value, (lax.axis_size(axis), *value.shape))
    return lax.all_to_all(copies, axis, 0, 0, tiled=True)


def to_all(value, axis):
    return lax.all_to_all(value, axis, 0, 0, tiled=True)


def local(impression_vectors, advertiser_vectors, spend_limits, capacity, blocks, counts):
    features = impression_vectors.shape[0]
    groups, _, slots = blocks.shape
    n_imp, n_adv = lax.axis_size(IMP), lax.axis_size(ADV)
    ids = blocks.reshape(groups, slots) // n_adv
    viewers_t = impression_vectors.T
    caps = capacity.reshape(groups, GROUP)
    catalog = spread(advertiser_vectors, IMP)
    spend = spread(spend_limits.reshape(1, BLOCK), IMP).reshape(n_imp, BLOCK)
    rate = 1.0 / spend

    exchange = (
        jax.ShapeDtypeStruct((n_imp, n_imp, BLOCK), F32),
        jax.ShapeDtypeStruct((groups, GROUP), F32),
    )
    priced = (jax.ShapeDtypeStruct((n_imp, BLOCK), F32),)
    scratch = [pltpu.VMEM((n_imp, 8, BLOCK), F32)]

    outlays, demand = pl.pallas_call(
        functools.partial(totals_kernel, True),
        in_specs=[SMEM, SMEM, VMEM, VMEM],
        out_specs=(VMEM, VMEM),
        out_shape=exchange,
        scratch_shapes=scratch,
        compiler_params=PARAMS,
    )(ids, counts, catalog, viewers_t)
    prices = jnp.zeros((n_imp, BLOCK), F32)
    duals = jnp.zeros((groups, GROUP), F32)

    def meet(outlays, demand, duals):
        outlays = to_all(outlays, IMP)
        pair = lax.all_gather(demand, "core", axis=0)
        demand = lax.psum((pair[0] + pair[1]).reshape(-1), "y").reshape(demand.shape)
        duals = jnp.maximum(duals + demand / caps - 1.0, 0.0)
        return outlays, duals

    for _ in range(2):
        outlays, duals = meet(outlays, demand, duals)
        outlays, demand, prices = pl.pallas_call(
            functools.partial(totals_kernel, False),
            in_specs=[SMEM, SMEM] + [VMEM] * 6,
            out_specs=(VMEM,) * 3,
            out_shape=exchange + priced,
            scratch_shapes=scratch,
            compiler_params=PARAMS,
        )(ids, counts, catalog, viewers_t, outlays, prices, rate, duals)
    outlays, duals = meet(outlays, demand, duals)
    imp_parts, adv_parts, prices = pl.pallas_call(
        grads_kernel,
        in_specs=[SMEM, SMEM] + [VMEM] * 7,
        out_specs=(VMEM,) * 3,
        out_shape=(
            jax.ShapeDtypeStruct((groups, features, GROUP), BF16),
            jax.ShapeDtypeStruct((n_imp, features, BLOCK), BF16),
        )
        + priced,
        scratch_shapes=[pltpu.VMEM((n_imp, features, BLOCK), F32)],
        compiler_params=PARAMS,
    )(ids, counts, catalog, viewers_t, impression_vectors, outlays, prices, rate, duals)
    adv_parts = to_all(adv_parts, IMP)
    imp_parts = to_all(imp_parts, ADV)
    impression_grad = jnp.sum(imp_parts.astype(F32), axis=0).astype(BF16)
    own_prices = lax.dynamic_index_in_dim(prices, lax.axis_index(IMP), 0, keepdims=False)
    advertiser_grad = jnp.sum(adv_parts.astype(F32), axis=0).astype(BF16)
    return own_prices, duals.reshape(-1), impression_grad, advertiser_grad


def solution(mesh):
    n_imp, n_adv = (mesh.shape[axis] for axis in ("imp", "adv"))
    chips = jax.sharding.Mesh(mesh.devices.reshape(n_imp // 4, 4, n_adv // 2, 2), IMP + ADV)
    return jax.shard_map(
        local,
        mesh=chips,
        in_specs=(
            P(None, IMP),
            P(None, IMP + ADV),
            P(IMP + ADV),
            P(IMP),
            P(IMP, ADV, None),
            P(IMP, ADV),
        ),
        out_specs=(P(IMP + ADV), P(IMP), P(None, IMP + ADV), P(None, IMP + ADV)),
        check_vma=False,
    )
```

time: 1180 us -> 205 us (0.17)
  the two profiles are of different devices: /device:TPU:29 before, /device:TPU:1 now
where the time goes in v1:
time: 205 us; the launch traced here: 204 us
  blocking collectives  74 us (36%)
  starting transfers between devices  54.4 us (27%)
  Pallas kernels  35.5 us (17%)
  waiting for transfers between devices  33 us (16%)
  local copies, waits for them, and re-layouts  3.84 us (2%)
    psum x3, blocking collectives, meet(): lax.psum((pair[0] + pair[1]).reshape(-1), 'y').reshape(demand.shape)  40.6 us
    all_to_all x4, starting transfers between devices, to_all(): return lax.all_to_all(value, axis, 0, 0, tiled=True)  35.3 us
    all_to_all x2, starting transfers between devices, spread(): return lax.all_to_all(copies, axis, 0, 0, tiled=True)  19.1 us
    all_to_all x1, blocking collectives, to_all(): return lax.all_to_all(value, axis, 0, 0, tiled=True)  18.6 us
    all_to_all x2, waiting for transfers between devices, spread(): return lax.all_to_all(copies, axis, 0, 0, tiled=True)  17.5 us
    pallas_call x1, Pallas kernels, local(): pl.pallas_call(grads_kernel, in_specs=[SMEM, SMEM] + [VMEM] * 7, out_spec...  15.6 us
    all_to_all x4, waiting for transfers between devices, to_all(): return lax.all_to_all(value, axis, 0, 0, tiled=True)  15.6 us
    all_gather x3, blocking collectives, meet(): pair = lax.all_gather(demand, 'core', axis=0)  14.7 us
  transfers between devices with their start and end apart: 6, of which 3 were waited for; matrix products, arithmetic and copies ran while one was open for 1% of the time, Pallas kernels for 3%

profile of v1, /device:TPU:1, one launch (start us, length us, event | category | flops | bytes accessed | tf_op | source)
XLA Modules:
  0.0 203.6 jit_solution(9210647004836422882)
XLA Ops:
  0.6 1.6 broadcast_in_dim.9
  2.3 0.0 copy-start.2
  2.3 0.0 copy-start
  2.3 13.8 %all-to-all-start = ((bf16[32,64,128]{2,1,0:T(8,128)(2,1)}), bf16[32,64,128]{2,1,0:T(8,128)(2,1)S(1)}, u32[]{:S(2)}, u32[]{:S(2)}) async-start(bf16[32,64,128]{2,1,0:T(8,128)(2,1)} %broadcast_in_dim.9), calls=%async_computation | async-start | bytes 1048576 | tf_op jit(solution)/shard_map/all_to_all | solution.py:116
  16.1 0.0 copy-done.2
  16.1 0.0 copy-start.3
  16.1 0.1 copy.19
  16.2 16.2 %all-to-all-done.catalog = bf16[32,64,128]{2,1,0:T(8,128)(2,1)S(1)} async-done(((bf16[32,64,128]{2,1,0:T(8,128)(2,1)}), bf16[32,64,128]{2,1,0:T(8,128)(2,1)S(1)}, u32[]{:S(2)}, u32[]{:S(2)}) %all-to-all-start) | async-done | bytes 524320 | tf_op jit(solution)/shard_map/all_to_all | solution.py:116
  32.4 0.0 copy-done.3
  32.4 0.6 broadcast_in_dim.11
  33.0 5.3 %all-to-all-start.2 = ((f32[32,1,128]{2,1,0:T(1,128)}), f32[32,1,128]{2,1,0:T(1,128)S(1)}, u32[]{:S(2)}, u32[]{:S(2)}) async-start(f32[32,1,128]{2,1,0:T(1,128)} %broadcast_in_dim.11), calls=%async_computation.2 | async-start | bytes 32768 | tf_op jit(solution)/shard_map/all_to_all | solution.py:116
  38.3 0.0 copy-start.4
  38.3 0.6 copy-done.4
  38.9 0.1 copy.28.counts
  39.0 0.0 copy-done
  39.0 0.3 copy.23
  39.3 6.2 %shard_map.93 = (f32[32,32,128]{2,1,0:T(8,128)}, f32[16,128]{1,0:T(8,128)S(1)}) custom-call(s32[16,8]{1,0:T(8,128)S(1)} %add_select_fusion.ids, s32[16,1]{1,0:T(8,128)S(1)} %copy.28.counts, bf16[32,64,128]{2,1,0:T(8,128)(2,1)S(1)} %all-to-all-done.catalog, bf16[2048,64]{1,0:T(8,128)(2,1)S(1)} %bitcast.32), custom_call_target="tpu_custom_call" | custom-call | tf_op jit(solution)/shard_map/pallas_call | solution.py:141
  45.5 1.3 all-to-all-done.2
  46.8 8.0 %all-to-all-start.1 = ((f32[32,32,128]{2,1,0:T(8,128)}), f32[32,32,128]{2,1,0:T(8,128)S(1)}, u32[]{:S(2)}, u32[]{:S(2)}) async-start(f32[32,32,128]{2,1,0:T(8,128)} %get-tuple-element.15), calls=%async_computation.1 | async-start | bytes 1048576 | tf_op jit(solution)/shard_map/all_to_all | solution.py:120
  54.9 3.8 %all-gather = f32[32,128]{1,0:T(8,128)S(1)} all-gather(f32[16,128]{1,0:T(8,128)S(1)} %get-tuple-element.16), channel_id=2, replica_groups=mesh['z'=8,'x'=4,'y'=8,'core'=2] {'core'}, dimensions={0}, use_global_device_ids=true | all-gather | bytes 24576 | tf_op jit(solution)/shard_map/all_gather | solution.py:154
  58.7 0.0 copy-start.1
  58.7 15.0 %psum.21 = f32[2048]{0:T(1024)S(1)} all-reduce(f32[2048]{0:T(1024)S(1)} %fusion.3), channel_id=1, replica_groups=mesh['z'=8,'x'=4,'y'=8,'core'=2] {'y'}, use_global_device_ids=true, to_apply=%region_0.1 | all-reduce | flops 2048 | bytes 16384 | tf_op jit(solution)/shard_map/psum | solution.py:155
  73.7 0.0 copy-done.1
  73.7 0.0 all-to-all-done.1.refs_0_
  73.8 6.8 %shard_map.94 = (f32[32,32,128]{2,1,0:T(8,128)}, f32[16,128]{1,0:T(8,128)S(1)}, f32[32,128]{1,0:T(8,128)S(1)}) custom-call(s32[16,8]{1,0:T(8,128)S(1)} %add_select_fusion.ids, s32[16,1]{1,0:T(8,128)S(1)} %copy.28.counts, bf16[32,64,128]{2,1,0:T(8,128)(2,1)S(1)} %all-to-all-done.catalog, bf16[2048,64]{1,0:T(8,128)(2,1)S(1)} %bitcast.33, ...), custom_call_target="tpu_custom_call" | custom-call | tf_op jit(solution)/shard_map/pallas_call | solution.py:161
  80.6 8.9 %all-to-all-start.3 = ((f32[32,32,128]{2,1,0:T(8,128)}), f32[32,32,128]{2,1,0:T(8,128)S(1)}, u32[]{:S(2)}, u32[]{:S(2)}) async-start(f32[32,32,128]{2,1,0:T(8,128)} %get-tuple-element.17), calls=%async_computation.3 | async-start | bytes 1048576 | tf_op jit(solution)/shard_map/all_to_all | solution.py:120
  89.5 5.6 %all-gather.1 = f32[32,128]{1,0:T(8,128)S(1)} all-gather(f32[16,128]{1,0:T(8,128)S(1)} %get-tuple-element.19), channel_id=3, replica_groups=mesh['z'=8,'x'=4,'y'=8,'core'=2] {'core'}, dimensions={0}, use_global_device_ids=true | all-gather | bytes 24576 | tf_op jit(solution)/shard_map/all_gather | solution.py:154
  95.1 12.6 %psum.22 = f32[2048]{0:T(1024)S(1)} all-reduce(f32[2048]{0:T(1024)S(1)} %fusion.2), channel_id=1, replica_groups=mesh['z'=8,'x'=4,'y'=8,'core'=2] {'y'}, use_global_device_ids=true, to_apply=%region_1.2 | all-reduce | flops 2048 | bytes 16384 | tf_op jit(solution)/shard_map/psum | solution.py:155
  107.7 0.0 all-to-all-done.3.refs_0_
  107.7 6.8 %shard_map.95 = (f32[32,32,128]{2,1,0:T(8,128)}, f32[16,128]{1,0:T(8,128)S(1)}, f32[32,128]{1,0:T(8,128)S(1)}) custom-call(s32[16,8]{1,0:T(8,128)S(1)} %add_select_fusion.ids, s32[16,1]{1,0:T(8,128)S(1)} %copy.28.counts, bf16[32,64,128]{2,1,0:T(8,128)(2,1)S(1)} %all-to-all-done.catalog, bf16[2048,64]{1,0:T(8,128)(2,1)S(1)} %bitcast.34, ...), custom_call_target="tpu_custom_call" | custom-call | tf_op jit(solution)/shard_map/pallas_call | solution.py:161
  114.6 8.9 %all-to-all-start.4 = ((f32[32,32,128]{2,1,0:T(8,128)}), f32[32,32,128]{2,1,0:T(8,128)S(1)}, u32[]{:S(2)}, u32[]{:S(2)}) async-start(f32[32,32,128]{2,1,0:T(8,128)} %get-tuple-element.20), calls=%async_computation.4 | async-start | bytes 1048576 | tf_op jit(solution)/shard_map/all_to_all | solution.py:120
  123.5 5.3 %all-gather.2 = f32[32,128]{1,0:T(8,128)S(1)} all-gather(f32[16,128]{1,0:T(8,128)S(1)} %get-tuple-element.22), channel_id=4, replica_groups=mesh['z'=8,'x'=4,'y'=8,'core'=2] {'core'}, dimensions={0}, use_global_device_ids=true | all-gather | bytes 24576 | tf_op jit(solution)/shard_map/all_gather | solution.py:154
  128.8 13.0 %psum.23 = f32[2048]{0:T(1024)S(1)} all-reduce(f32[2048]{0:T(1024)S(1)} %fusion.1), channel_id=1, replica_groups=mesh['z'=8,'x'=4,'y'=8,'core'=2] {'y'}, use_global_device_ids=true, to_apply=%region_2.3 | all-reduce | flops 2048 | bytes 16384 | tf_op jit(solution)/shard_map/psum | solution.py:155
  141.8 0.0 all-to-all-done.4.outlays
  141.8 15.6 %shard_map.96 = (bf16[16,64,128]{2,1,0:T(8,128)(2,1)S(1)}, bf16[32,64,128]{2,1,0:T(8,128)(2,1)}, f32[32,128]{1,0:T(8,128)S(1)}) custom-call(s32[16,8]{1,0:T(8,128)S(1)} %add_select_fusion.ids, s32[16,1]{1,0:T(8,128)S(1)} %copy.28.counts, bf16[32,64,128]{2,1,0:T(8,128)(2,1)S(1)} %all-to-all-done.catalog, bf16[2048,64]{1,0:T(8,128)(2,1)S(1)} %bitcast.35, ...), custom_call_target="tpu_custom_call" | custom-call | tf_op jit(solution)/shard_map/pallas_call | solution.py:170
  157.4 18.6 %all_to_all.35 = bf16[16,64,128]{2,1,0:T(8,128)(2,1)S(1)} all-to-all(bf16[16,64,128]{2,1,0:T(8,128)(2,1)S(1)} %get-tuple-element.24), channel_id=1, replica_groups=mesh['z'=8,'x'=4,'y'=8,'core'=2] {'y','core'}, dimensions={0} | all-to-all | bytes 524288 | tf_op jit(solution)/shard_map/all_to_all | solution.py:120
  176.1 9.5 %all-to-all-start.6 = ((bf16[32,64,128]{2,1,0:T(8,128)(2,1)}), bf16[32,64,128]{2,1,0:T(8,128)(2,1)S(1)}, u32[]{:S(2)}, u32[]{:S(2)}) async-start(bf16[32,64,128]{2,1,0:T(8,128)(2,1)} %get-tuple-element.25), calls=%async_computation.6 | async-start | bytes 1048576 | tf_op jit(solution)/shard_map/all_to_all | solution.py:120
  185.6 0.6 add_maximum_fusion
  186.2 0.5 dynamic-slice_bitcast_fusion
  186.7 0.6 reduce_sum.24
  187.4 15.6 %all-to-all-done.6 = bf16[32,64,128]{2,1,0:T(8,128)(2,1)S(1)} async-done(((bf16[32,64,128]{2,1,0:T(8,128)(2,1)}), bf16[32,64,128]{2,1,0:T(8,128)(2,1)S(1)}, u32[]{:S(2)}, u32[]{:S(2)}) %all-to-all-start.6) | async-done | bytes 524320 | tf_op jit(solution)/shard_map/all_to_all | solution.py:120
  202.9 0.7 reduce_sum.25
  (9 shorter events, 0.1 us)
Async XLA Ops:
  2.3 13.8 %copy-start.2 = (s32[16,1,8]{0,2,1:T(8,128)S(1)}, s32[16,1,8]{0,2,1:T(8,128)}, u32[]{:S(2)}) copy-start(s32[16,1,8]{0,2,1:T(8,128)} %param.10) | copy-start | bytes 1540
  2.3 36.8 %copy-start = (bf16[64,2048]{1,0:T(8,128)(2,1)S(1)}, bf16[64,2048]{1,0:T(8,128)(2,1)}, u32[]{:S(2)}) copy-start(bf16[64,2048]{1,0:T(8,128)(2,1)} %viewers.1) | copy-start | bytes 786436
  2.3 30.1 %all-to-all-start = ((bf16[32,64,128]{2,1,0:T(8,128)(2,1)}), bf16[32,64,128]{2,1,0:T(8,128)(2,1)S(1)}, u32[]{:S(2)}, u32[]{:S(2)}) async-start(bf16[32,64,128]{2,1,0:T(8,128)(2,1)} %broadcast_in_dim.9), calls=%async_computation | async-start | bytes 1048576 | tf_op jit(solution)/shard_map/all_to_all | solution.py:116
  16.1 16.3 %copy-start.3 = (f32[128]{0:T(128)S(1)}, f32[128]{0:T(128)}, u32[]{:S(2)}) copy-start(f32[128]{0:T(128)} %param.8) | copy-start | bytes 1540
  33.0 13.8 %all-to-all-start.2 = ((f32[32,1,128]{2,1,0:T(1,128)}), f32[32,1,128]{2,1,0:T(1,128)S(1)}, u32[]{:S(2)}, u32[]{:S(2)}) async-start(f32[32,1,128]{2,1,0:T(1,128)} %broadcast_in_dim.11), calls=%async_computation.2 | async-start | bytes 32768 | tf_op jit(solution)/shard_map/all_to_all | solution.py:116
  38.3 0.7 copy-start.4
  46.8 26.9 %all-to-all-start.1 = ((f32[32,32,128]{2,1,0:T(8,128)}), f32[32,32,128]{2,1,0:T(8,128)S(1)}, u32[]{:S(2)}, u32[]{:S(2)}) async-start(f32[32,32,128]{2,1,0:T(8,128)} %get-tuple-element.15), calls=%async_computation.1 | async-start | bytes 1048576 | tf_op jit(solution)/shard_map/all_to_all | solution.py:120
  58.7 15.0 %copy-start.1 = (f32[2048]{0:T(1024)S(1)}, f32[2048]{0:T(1024)}, u32[]{:S(2)}) copy-start(f32[2048]{0:T(1024)} %param.9) | copy-start | bytes 24580
  80.6 27.1 %all-to-all-start.3 = ((f32[32,32,128]{2,1,0:T(8,128)}), f32[32,32,128]{2,1,0:T(8,128)S(1)}, u32[]{:S(2)}, u32[]{:S(2)}) async-start(f32[32,32,128]{2,1,0:T(8,128)} %get-tuple-element.17), calls=%async_computation.3 | async-start | bytes 1048576 | tf_op jit(solution)/shard_map/all_to_all | solution.py:120
  114.6 27.2 %all-to-all-start.4 = ((f32[32,32,128]{2,1,0:T(8,128)}), f32[32,32,128]{2,1,0:T(8,128)S(1)}, u32[]{:S(2)}, u32[]{:S(2)}) async-start(f32[32,32,128]{2,1,0:T(8,128)} %get-tuple-element.20), calls=%async_computation.4 | async-start | bytes 1048576 | tf_op jit(solution)/shard_map/all_to_all | solution.py:120
  176.1 26.8 %all-to-all-start.6 = ((bf16[32,64,128]{2,1,0:T(8,128)(2,1)}), bf16[32,64,128]{2,1,0:T(8,128)(2,1)S(1)}, u32[]{:S(2)}, u32[]{:S(2)}) async-start(bf16[32,64,128]{2,1,0:T(8,128)(2,1)} %get-tuple-element.25), calls=%async_computation.6 | async-start | bytes 1048576 | tf_op jit(solution)/shard_map/all_to_all | solution.py:120

commit v2 on v1

v2 whole, which is shorter than its diff:
```python
import functools

import jax
import jax.numpy as jnp
from jax import lax
from jax.experimental import pallas as pl
from jax.experimental.pallas import tpu as pltpu
from jax.sharding import PartitionSpec as P


GROUP = 128
BLOCK = 128
PARTS = 8
STRIP = 16
UNROLL = 2
DEAD = 1e30

F32 = jnp.float32
BF16 = jnp.bfloat16
IMP = ("z", "x")
ADV = ("y", "core")
VMEM = pl.BlockSpec(memory_space=pltpu.VMEM)
SMEM = pl.BlockSpec(memory_space=pltpu.SMEM)
PARAMS = pltpu.CompilerParams(vmem_limit_bytes=16 << 20)


def parts_of(value):
    high = value.astype(BF16).astype(F32)
    rest = value - high
    middle = rest.astype(BF16).astype(F32)
    return high, middle, rest - middle


def rows_of(rows, count):
    place = lax.broadcasted_iota(jnp.int32, (count, rows[0].shape[1]), 0)
    stacked = jnp.zeros((count, rows[0].shape[1]), F32)
    for index, row in enumerate(rows):
        stacked = jnp.where(place == index, row, stacked)
    return stacked


def pack_kernel(vectors, spend, out):
    features = vectors.shape[0]
    columns = vectors[...]
    limits = rows_of(parts_of(spend[...]), PARTS).astype(BF16)
    for peer in range(out.shape[0]):
        out[peer, :features, :] = columns
        out[peer, features:, :] = limits


def new_prices(outlays, old_prices, rate):
    return jnp.maximum(old_prices[...] + jnp.sum(outlays[...], axis=0) * rate[...] - 1.0, 0.0)


def set_strips(strips, prices):
    blocks = strips.shape[0] - 1
    strips[...] = jnp.zeros_like(strips)
    dead = jnp.full((1, BLOCK), -DEAD, F32)
    strips[blocks, :, :] = rows_of([dead], STRIP).astype(BF16)
    if prices is not None:
        parts = parts_of(-prices)
        for block in range(blocks):
            rows = rows_of([part[block : block + 1, :] for part in parts], 8)
            rows = jnp.concatenate([rows, jnp.zeros((STRIP - 8, BLOCK), F32)], axis=0)
            strips[block, :, :] = rows.astype(BF16)


def turned_duals(duals, width):
    parts = parts_of(duals)
    above = jnp.zeros((width - 3 * duals.shape[0], GROUP), F32)
    return jnp.concatenate([above, *parts], axis=0).T.astype(BF16)


def pair_shares(group_no, slot, ids, catalog, strips, viewer, groups, duals):
    features = catalog.shape[1] - PARTS
    last = catalog.shape[0] - 1
    first, second = ids[group_no, slot], ids[group_no, slot + 1]
    vectors = jnp.concatenate(
        [
            catalog[jnp.minimum(first, last), :features, :],
            catalog[jnp.minimum(second, last), :features, :],
        ],
        axis=1,
    )
    rows = [vectors, jnp.concatenate([strips[first], strips[second]], axis=1)]
    if duals:
        place = lax.broadcasted_iota(jnp.int32, (groups, 2 * BLOCK), 0)
        rows += [jnp.where(place == group_no, -1.0, 0.0).astype(BF16)] * 3
    scores = jnp.dot(viewer, jnp.concatenate(rows, axis=0), preferred_element_type=F32)
    return jnp.clip(scores, 0.0, 1.0), vectors, first, second


def totals_kernel(first_pass, ids, catalog, viewers_t, *refs):
    groups, slots = ids.shape
    features = catalog.shape[1] - PARTS
    if first_pass:
        outlay_out, demand_out, rate, strips, outlay_acc, demand_acc = refs
        limits = catalog[:, features:, :].astype(F32)
        rate[...] = 1.0 / jnp.sum(limits, axis=1)
        set_strips(strips, None)
    else:
        (outlays, old_prices, rate, duals,
         outlay_out, demand_out, prices, strips, outlay_acc, demand_acc) = refs
        prices[...] = new_prices(outlays, old_prices, rate)
        set_strips(strips, prices[...])
        turned = turned_duals(duals[...], viewers_t.shape[1])
    outlay_acc[...] = jnp.zeros_like(outlay_acc)
    demand_acc[...] = jnp.zeros_like(demand_acc)
    lane = lax.broadcasted_iota(jnp.int32, (GROUP, BLOCK), 1)

    def step(group_no, _):
        start = pl.multiple_of(group_no * GROUP, GROUP)
        viewer = viewers_t[pl.ds(start, GROUP), :]
        viewer = viewer[:, : features + STRIP] if first_pass else viewer + turned
        by_viewer = jnp.zeros((GROUP, BLOCK), F32)
        for slot in range(0, slots, 2):
            shares, _, first, second = pair_shares(
                group_no, slot, ids, catalog, strips, viewer, groups, not first_pass
            )
            by_viewer = by_viewer + (shares[:, :BLOCK] + shares[:, BLOCK:])
            folded = jnp.sum(shares.reshape(GROUP // 8, 8, 2 * BLOCK), axis=0)
            outlay_acc[first] += folded[:, :BLOCK]
            outlay_acc[second] += folded[:, BLOCK:]
        demand = jnp.sum(by_viewer, axis=1, keepdims=True)
        demand_acc[...] = jnp.where(lane == group_no, demand, demand_acc[...])
        return 0

    lax.fori_loop(0, groups, step, 0, unroll=UNROLL)
    demand_out[...] = demand_acc[...].T[:groups, :]
    peers = outlay_out.shape[0]
    outlay = jnp.sum(outlay_acc[:peers], axis=1)
    for peer in range(peers):
        outlay_out[peer] = outlay


def adv_kernel(
    ids, own, catalog, viewers_t, viewers, outlays, old_prices, rate, duals,
    adv_out, own_prices, duals_out, strips_out, adv_acc, prices,
):
    groups, slots = ids.shape
    prices[...] = new_prices(outlays, old_prices, rate)
    own_prices[...] = prices[pl.ds(own[0], 1), :]
    duals_out[...] = duals[...]
    set_strips(strips_out, prices[...])
    turned = turned_duals(duals[...], viewers_t.shape[1])
    adv_acc[...] = jnp.zeros_like(adv_acc)

    def step(group_no, _):
        start = pl.multiple_of(group_no * GROUP, GROUP)
        viewer_t = viewers_t[pl.ds(start, GROUP), :] + turned
        viewer = viewers[:, pl.ds(start, GROUP)]
        for slot in range(0, slots, 2):
            shares, _, first, second = pair_shares(
                group_no, slot, ids, catalog, strips_out, viewer_t, groups, True
            )
            terms = jnp.dot(viewer, shares.astype(BF16), preferred_element_type=F32)
            adv_acc[first] += terms[:, :BLOCK]
            adv_acc[second] += terms[:, BLOCK:]
        return 0

    lax.fori_loop(0, groups, step, 0, unroll=UNROLL)
    adv_out[...] = (adv_acc[: adv_out.shape[0]] * (1.0 / GROUP)).astype(BF16)


def imp_kernel(ids, catalog, viewers_t, strips, duals, imp_out):
    groups, slots = ids.shape
    features = catalog.shape[1] - PARTS
    turned = turned_duals(duals[...], viewers_t.shape[1])

    def step(group_no, _):
        start = pl.multiple_of(group_no * GROUP, GROUP)
        viewer_t = viewers_t[pl.ds(start, GROUP), :] + turned
        imp_part = jnp.zeros((features, GROUP), F32)
        for slot in range(0, slots, 2):
            shares, vectors, _, _ = pair_shares(
                group_no, slot, ids, catalog, strips, viewer_t, groups, True
            )
            imp_part = imp_part + lax.dot_general(
                vectors, shares.astype(BF16), (((1,), (1,)), ((), ())),
                preferred_element_type=F32,
            )
        imp_out[lax.rem(group_no, 2), lax.div(group_no, 2)] = imp_part.astype(BF16)
        return 0

    lax.fori_loop(0, groups, step, 0, unroll=UNROLL)


def to_all(value, axis):
    return lax.all_to_all(value, axis, 0, 0, tiled=True)


def call(kernel, n_smem, out_shape, scratch, *args):
    return pl.pallas_call(
        kernel,
        in_specs=[SMEM] * n_smem + [VMEM] * (len(args) - n_smem),
        out_specs=(VMEM,) * len(out_shape),
        out_shape=tuple(jax.ShapeDtypeStruct(shape, dtype) for shape, dtype in out_shape),
        scratch_shapes=[pltpu.VMEM(shape, dtype) for shape, dtype in scratch],
        compiler_params=PARAMS,
    )(*args)


def local(impression_vectors, advertiser_vectors, spend_limits, capacity, blocks, counts):
    features = impression_vectors.shape[0]
    groups, _, slots = blocks.shape
    n_imp, n_adv = lax.axis_size(IMP), lax.axis_size(ADV)
    live = jnp.arange(slots)[None, :] < counts
    ids = jnp.where(live, blocks.reshape(groups, slots) // n_adv, n_imp)
    own = lax.axis_index(IMP).astype(jnp.int32).reshape(1)
    caps = capacity.reshape(groups, GROUP)
    ones = jnp.ones((3, impression_vectors.shape[1]), BF16)
    rest = STRIP - 3 + 3 * groups
    zeros = jnp.zeros((rest, impression_vectors.shape[1]), BF16)
    viewers_t = jnp.concatenate([impression_vectors, ones, zeros], axis=0).T

    (packed,) = call(
        pack_kernel, 0, [((n_imp, features + PARTS, BLOCK), BF16)], [],
        advertiser_vectors, spend_limits.reshape(1, BLOCK),
    )
    catalog = to_all(packed, IMP)

    exchange = [((n_imp, n_imp, BLOCK), F32), ((groups, GROUP), F32)]
    levels = [((n_imp, BLOCK), F32)]
    strips = [((n_imp + 1, STRIP, BLOCK), BF16)]
    sums = [((n_imp + 1, 8, BLOCK), F32), ((GROUP, BLOCK), F32)]

    outlays, demand, rate = call(
        functools.partial(totals_kernel, True), 1, exchange + levels, strips + sums,
        ids, catalog, viewers_t,
    )
    prices = jnp.zeros((n_imp, BLOCK), F32)
    duals = jnp.zeros((groups, GROUP), F32)

    def meet(outlays, demand, duals):
        outlays = to_all(outlays, IMP)
        pair = lax.all_gather(demand, "core", axis=0)
        demand = lax.psum((pair[0] + pair[1]).reshape(-1), "y").reshape(demand.shape)
        duals = jnp.maximum(duals + demand / caps - 1.0, 0.0)
        return outlays, duals

    for _ in range(2):
        outlays, duals = meet(outlays, demand, duals)
        outlays, demand, prices = call(
            functools.partial(totals_kernel, False), 1, exchange + levels,
            strips + sums,
            ids, catalog, viewers_t, outlays, prices, rate, duals,
        )
    outlays, duals = meet(outlays, demand, duals)
    adv_parts, own_prices, out_duals, strip_rows = call(
        adv_kernel, 2,
        [
            ((n_imp, features, BLOCK), BF16),
            ((1, BLOCK), F32),
            ((groups, GROUP), F32),
            *strips,
        ],
        [((n_imp + 1, features, BLOCK), F32)] + levels,
        ids, own, catalog, viewers_t, impression_vectors, outlays, prices, rate, duals,
    )
    adv_parts = to_all(adv_parts, IMP)
    (imp_parts,) = call(
        imp_kernel, 1, [((2, groups // 2, features, GROUP), BF16)], [],
        ids, catalog, viewers_t, strip_rows, duals,
    )
    core = lax.axis_index("core")
    kept = lax.dynamic_index_in_dim(imp_parts, core, 0, keepdims=False)
    given = lax.dynamic_index_in_dim(imp_parts, 1 - core, 0, keepdims=False)
    given = lax.ppermute(given, "core", [(0, 1), (1, 0)])
    imp_parts = (kept.astype(F32) + given.astype(F32)).astype(BF16)
    imp_parts = to_all(imp_parts, "y")
    impression_grad = jnp.sum(imp_parts.astype(F32), axis=0).astype(BF16)
    advertiser_grad = jnp.sum(adv_parts.astype(F32), axis=0).astype(BF16)
    return own_prices.reshape(-1), out_duals.reshape(-1), impression_grad, advertiser_grad


def solution(mesh):
    n_imp, n_adv = (mesh.shape[axis] for axis in ("imp", "adv"))
    chips = jax.sharding.Mesh(mesh.devices.reshape(n_imp // 4, 4, n_adv // 2, 2), IMP + ADV)
    return jax.shard_map(
        local,
        mesh=chips,
        in_specs=(
            P(None, IMP),
            P(None, IMP + ADV),
            P(IMP + ADV),
            P(IMP),
            P(IMP, ADV, None),
            P(IMP, ADV),
        ),
        out_specs=(P(IMP + ADV), P(IMP), P(None, IMP + ADV), P(None, IMP + ADV)),
        check_vma=False,
    )
```

time: 205 us -> 192 us (0.937)
  the two profiles are of different devices: /device:TPU:1 before, /device:TPU:2 now
where the time goes in v2:
time: 192 us; the launch traced here: 191 us
  blocking collectives  67.7 us (35%)
  starting transfers between devices  50.4 us (26%)
  Pallas kernels  34.7 us (18%)
  waiting for transfers between devices  32.4 us (17%)
  local copies, waits for them, and re-layouts  3.08 us (2%)
    psum x3, blocking collectives, meet(): lax.psum((pair[0] + pair[1]).reshape(-1), 'y').reshape(demand.shape)  48.7 us
    all_to_all x5, starting transfers between devices, to_all(): return lax.all_to_all(value, axis, 0, 0, tiled=True)  48.5 us
    pallas_call x6, Pallas kernels, call(): pl.pallas_call(kernel, in_specs=[SMEM] * n_smem + [VMEM] * (len(args) - n...  34.7 us
    all_to_all x5, waiting for transfers between devices, to_all(): return lax.all_to_all(value, axis, 0, 0, tiled=True)  31 us
    all_to_all x1, blocking collectives, to_all(): return lax.all_to_all(value, axis, 0, 0, tiled=True)  13.5 us
    all_gather x3, blocking collectives, meet(): pair = lax.all_gather(demand, 'core', axis=0)  5.46 us
  transfers between devices with their start and end apart: 6, of which 3 were waited for; matrix products, arithmetic and copies ran while one was open for 1% of the time, Pallas kernels for 0%

profile of v2, /device:TPU:2, one launch (start us, length us, event | category | flops | bytes accessed | tf_op | source)
XLA Modules:
  0.0 190.7 jit_solution(11154781986565983776)
XLA Ops:
  0.6 0.0 copy-start.2
  0.6 0.6 copy-done.2
  1.3 0.0 copy-start.1
  1.3 0.7 copy-done.1
  2.0 0.9 shard_map.93
  2.9 0.0 copy-start
  2.9 13.6 %all-to-all-start = ((bf16[32,72,128]{2,1,0:T(8,128)(2,1)}), bf16[32,72,128]{2,1,0:T(8,128)(2,1)S(1)}, u32[]{:S(2)}, u32[]{:S(2)}) async-start(bf16[32,72,128]{2,1,0:T(8,128)(2,1)} %shard_map.93), calls=%async_computation | async-start | bytes 1179648 | tf_op jit(solution)/shard_map/all_to_all | solution.py:189
  16.5 0.0 copy-done
  16.5 0.3 copy.14
  16.8 0.0 copy-start.4
  16.8 0.1 pad.1.clone
  16.9 0.1 pad.2.clone
  17.0 0.5 copy-done.4
  17.5 0.1 copy.10
  17.6 0.0 copy-start.5
  17.6 0.7 copy-done.5
  18.2 0.1 fusion.2.ids
  18.3 0.2 maximum_bitcast_fusion.viewers_t
  18.5 16.3 %all-to-all-done.catalog = bf16[32,72,128]{2,1,0:T(8,128)(2,1)S(1)} async-done(((bf16[32,72,128]{2,1,0:T(8,128)(2,1)}), bf16[32,72,128]{2,1,0:T(8,128)(2,1)S(1)}, u32[]{:S(2)}, u32[]{:S(2)}) %all-to-all-start) | async-done | bytes 589856 | tf_op jit(solution)/shard_map/all_to_all | solution.py:189
  34.8 4.5 %shard_map.94 = (f32[32,32,128]{2,1,0:T(8,128)}, f32[16,128]{1,0:T(8,128)S(1)}, f32[32,128]{1,0:T(8,128)S(1)}) custom-call(s32[16,8]{1,0:T(8,128)S(1)} %fusion.2.ids, bf16[32,72,128]{2,1,0:T(8,128)(2,1)S(1)} %all-to-all-done.catalog, bf16[2048,128]{1,0:T(8,128)(2,1)S(1)} %maximum_bitcast_fusion.viewers_t), custom_call_target="tpu_custom_call" | custom-call | tf_op jit(solution)/shard_map/pallas_call | solution.py:193
  39.3 5.6 %all-to-all-start.1 = ((f32[32,32,128]{2,1,0:T(8,128)}), f32[32,32,128]{2,1,0:T(8,128)S(1)}, u32[]{:S(2)}, u32[]{:S(2)}) async-start(f32[32,32,128]{2,1,0:T(8,128)} %get-tuple-element.17), calls=%async_computation.1 | async-start | bytes 1048576 | tf_op jit(solution)/shard_map/all_to_all | solution.py:189
  44.8 1.8 all-gather
  46.7 0.0 copy-start.3
  46.7 17.9 %psum.21 = f32[2048]{0:T(1024)S(1)} all-reduce(f32[2048]{0:T(1024)S(1)} %fusion.5), channel_id=1, replica_groups=mesh['z'=8,'x'=4,'y'=8,'core'=2] {'y'}, use_global_device_ids=true, to_apply=%region_0.1 | all-reduce | flops 2048 | bytes 16384 | tf_op jit(solution)/shard_map/psum | solution.py:237
  64.6 0.0 copy-done.3
  64.6 0.0 all-to-all-done.1.refs_0_
  64.6 4.7 %shard_map.95 = (f32[32,32,128]{2,1,0:T(8,128)}, f32[16,128]{1,0:T(8,128)S(1)}, f32[32,128]{1,0:T(8,128)S(1)}) custom-call(s32[16,8]{1,0:T(8,128)S(1)} %fusion.2.ids, bf16[32,72,128]{2,1,0:T(8,128)(2,1)S(1)} %all-to-all-done.catalog, bf16[2048,128]{1,0:T(8,128)(2,1)S(1)} %maximum_bitcast_fusion.viewers_t, f32[32,32,128]{2,1,0:T(8,128)S(1)} %all-to-all-done.1.refs_0_, ...), custom_call_target="tpu_custom_call" | custom-call | tf_op jit(solution)/shard_map/pallas_call | solution.py:193
  69.3 9.8 %all-to-all-start.2 = ((f32[32,32,128]{2,1,0:T(8,128)}), f32[32,32,128]{2,1,0:T(8,128)S(1)}, u32[]{:S(2)}, u32[]{:S(2)}) async-start(f32[32,32,128]{2,1,0:T(8,128)} %get-tuple-element.20), calls=%async_computation.2 | async-start | bytes 1048576 | tf_op jit(solution)/shard_map/all_to_all | solution.py:189
  79.1 1.8 all-gather.1
  80.9 15.2 %psum.22 = f32[2048]{0:T(1024)S(1)} all-reduce(f32[2048]{0:T(1024)S(1)} %fusion.4), channel_id=1, replica_groups=mesh['z'=8,'x'=4,'y'=8,'core'=2] {'y'}, use_global_device_ids=true, to_apply=%region_1.2 | all-reduce | flops 2048 | bytes 16384 | tf_op jit(solution)/shard_map/psum | solution.py:237
  96.1 0.0 all-to-all-done.2.refs_0_
  96.1 4.7 %shard_map.96 = (f32[32,32,128]{2,1,0:T(8,128)}, f32[16,128]{1,0:T(8,128)S(1)}, f32[32,128]{1,0:T(8,128)S(1)}) custom-call(s32[16,8]{1,0:T(8,128)S(1)} %fusion.2.ids, bf16[32,72,128]{2,1,0:T(8,128)(2,1)S(1)} %all-to-all-done.catalog, bf16[2048,128]{1,0:T(8,128)(2,1)S(1)} %maximum_bitcast_fusion.viewers_t, f32[32,32,128]{2,1,0:T(8,128)S(1)} %all-to-all-done.2.refs_0_, ...), custom_call_target="tpu_custom_call" | custom-call | tf_op jit(solution)/shard_map/pallas_call | solution.py:193
  100.8 9.8 %all-to-all-start.3 = ((f32[32,32,128]{2,1,0:T(8,128)}), f32[32,32,128]{2,1,0:T(8,128)S(1)}, u32[]{:S(2)}, u32[]{:S(2)}) async-start(f32[32,32,128]{2,1,0:T(8,128)} %get-tuple-element.23), calls=%async_computation.3 | async-start | bytes 1048576 | tf_op jit(solution)/shard_map/all_to_all | solution.py:189
  110.6 1.8 all-gather.2
  112.4 15.6 %psum.23 = f32[2048]{0:T(1024)S(1)} all-reduce(f32[2048]{0:T(1024)S(1)} %fusion.3), channel_id=1, replica_groups=mesh['z'=8,'x'=4,'y'=8,'core'=2] {'y'}, use_global_device_ids=true, to_apply=%region_2.3 | all-reduce | flops 2048 | bytes 16384 | tf_op jit(solution)/shard_map/psum | solution.py:237
  128.1 0.0 all-to-all-done.3.outlays
  128.1 13.6 %shard_map.97 = (bf16[32,64,128]{2,1,0:T(8,128)(2,1)}, f32[1,128]{1,0:T(1,128)}, f32[16,128]{1,0:T(8,128)}, bf16[33,16,128]{2,1,0:T(8,128)(2,1)S(1)}) custom-call(s32[16,8]{1,0:T(8,128)S(1)} %fusion.2.ids, s32[1]{0:T(128)} %bitcast.2.own, bf16[32,72,128]{2,1,0:T(8,128)(2,1)S(1)} %all-to-all-done.catalog, ...), custom_call_target="tpu_custom_call" | custom-call | tf_op jit(solution)/shard_map/pallas_call | solution.py:193
  141.7 6.3 %shard_map.98 = bf16[2,8,64,128]{3,2,1,0:T(8,128)(2,1)S(1)} custom-call(s32[16,8]{1,0:T(8,128)S(1)} %fusion.2.ids, bf16[32,72,128]{2,1,0:T(8,128)(2,1)S(1)} %all-to-all-done.catalog, bf16[2048,128]{1,0:T(8,128)(2,1)S(1)} %maximum_bitcast_fusion.viewers_t, bf16[33,16,128]{2,1,0:T(8,128)(2,1)S(1)} %get-tuple-element.28.strips, f32[16,128]{1,0:T(8,128)S(1)} %fusion.7.duals), custom_call_target="tpu_custom_call" | custom-call | tf_op jit(solution)/shard_map/pallas_call | solution.py:193
  148.0 1.9 %collective-permute-start = (bf16[8,64,128]{2,1,0:T(8,128)(2,1)S(1)}, bf16[8,64,128]{2,1,0:T(8,128)(2,1)S(1)}, u32[]{:S(2)}, u32[]{:S(2)}) collective-permute-start(bf16[8,64,128]{2,1,0:T(8,128)(2,1)S(1)} %dynamic-slice_bitcast_fusion), channel_id=1, source_target_pairs={{0,1},{1,0},{2,3},{3,2},{4,5},{5,4},{6,7},{7,6},{8,9},{9,8},{10,11... | collective-permute-start | bytes 393224 | tf_op jit(solution)/shard_map/ppermute | solution.py:268
  150.0 1.3 collective-permute-done
  151.3 13.5 %all_to_all.30 = bf16[8,64,128]{2,1,0:T(8,128)(2,1)S(1)} all-to-all(bf16[8,64,128]{2,1,0:T(8,128)(2,1)S(1)} %fusion), channel_id=1, replica_groups=mesh['z'=8,'x'=4,'y'=8,'core'=2] {'y'}, dimensions={0} | all-to-all | bytes 262144 | tf_op jit(solution)/shard_map/all_to_all | solution.py:189
  164.8 9.8 %all-to-all-start.5 = ((bf16[32,64,128]{2,1,0:T(8,128)(2,1)}), bf16[32,64,128]{2,1,0:T(8,128)(2,1)S(1)}, u32[]{:S(2)}, u32[]{:S(2)}) async-start(bf16[32,64,128]{2,1,0:T(8,128)(2,1)} %get-tuple-element.29), calls=%async_computation.5 | async-start | bytes 1048576 | tf_op jit(solution)/shard_map/all_to_all | solution.py:189
  174.6 0.6 reduce_sum.24
  175.2 14.8 %all-to-all-done.5 = bf16[32,64,128]{2,1,0:T(8,128)(2,1)S(1)} async-done(((bf16[32,64,128]{2,1,0:T(8,128)(2,1)}), bf16[32,64,128]{2,1,0:T(8,128)(2,1)S(1)}, u32[]{:S(2)}, u32[]{:S(2)}) %all-to-all-start.5) | async-done | bytes 524320 | tf_op jit(solution)/shard_map/all_to_all | solution.py:189
  190.0 0.7 reduce_sum.25
  (11 shorter events, 0.1 us)
Async XLA Ops:
  0.6 0.7 copy-start.2
  1.3 0.7 copy-start.1
  2.9 13.6 %copy-start = (bf16[64,2048]{1,0:T(8,128)(2,1)S(1)}, bf16[64,2048]{1,0:T(8,128)(2,1)}, u32[]{:S(2)}) copy-start(bf16[64,2048]{1,0:T(8,128)(2,1)} %viewers.1) | copy-start | bytes 786436
  2.9 31.8 %all-to-all-start = ((bf16[32,72,128]{2,1,0:T(8,128)(2,1)}), bf16[32,72,128]{2,1,0:T(8,128)(2,1)S(1)}, u32[]{:S(2)}, u32[]{:S(2)}) async-start(bf16[32,72,128]{2,1,0:T(8,128)(2,1)} %shard_map.93), calls=%async_computation | async-start | bytes 1179648 | tf_op jit(solution)/shard_map/all_to_all | solution.py:189
  16.8 0.7 copy-start.4
  17.6 0.7 copy-start.5
  39.3 25.3 %all-to-all-start.1 = ((f32[32,32,128]{2,1,0:T(8,128)}), f32[32,32,128]{2,1,0:T(8,128)S(1)}, u32[]{:S(2)}, u32[]{:S(2)}) async-start(f32[32,32,128]{2,1,0:T(8,128)} %get-tuple-element.17), calls=%async_computation.1 | async-start | bytes 1048576 | tf_op jit(solution)/shard_map/all_to_all | solution.py:189
  46.7 17.9 %copy-start.3 = (f32[2048]{0:T(1024)S(1)}, f32[2048]{0:T(1024)}, u32[]{:S(2)}) copy-start(f32[2048]{0:T(1024)} %param.9) | copy-start | bytes 24580
  69.3 26.9 %all-to-all-start.2 = ((f32[32,32,128]{2,1,0:T(8,128)}), f32[32,32,128]{2,1,0:T(8,128)S(1)}, u32[]{:S(2)}, u32[]{:S(2)}) async-start(f32[32,32,128]{2,1,0:T(8,128)} %get-tuple-element.20), calls=%async_computation.2 | async-start | bytes 1048576 | tf_op jit(solution)/shard_map/all_to_all | solution.py:189
  100.8 27.2 %all-to-all-start.3 = ((f32[32,32,128]{2,1,0:T(8,128)}), f32[32,32,128]{2,1,0:T(8,128)S(1)}, u32[]{:S(2)}, u32[]{:S(2)}) async-start(f32[32,32,128]{2,1,0:T(8,128)} %get-tuple-element.23), calls=%async_computation.3 | async-start | bytes 1048576 | tf_op jit(solution)/shard_map/all_to_all | solution.py:189
  148.0 3.2 %collective-permute-start = (bf16[8,64,128]{2,1,0:T(8,128)(2,1)S(1)}, bf16[8,64,128]{2,1,0:T(8,128)(2,1)S(1)}, u32[]{:S(2)}, u32[]{:S(2)}) collective-permute-start(bf16[8,64,128]{2,1,0:T(8,128)(2,1)S(1)} %dynamic-slice_bitcast_fusion), channel_id=1, source_target_pairs={{0,1},{1,0},{2,3},{3,2},{4,5},{5,4},{6,7},{7,6},{8,9},{9,8},{10,11... | collective-permute-start | bytes 393224 | tf_op jit(solution)/shard_map/ppermute | solution.py:268
  164.8 25.2 %all-to-all-start.5 = ((bf16[32,64,128]{2,1,0:T(8,128)(2,1)}), bf16[32,64,128]{2,1,0:T(8,128)(2,1)S(1)}, u32[]{:S(2)}, u32[]{:S(2)}) async-start(bf16[32,64,128]{2,1,0:T(8,128)(2,1)} %get-tuple-element.29), calls=%async_computation.5 | async-start | bytes 1048576 | tf_op jit(solution)/shard_map/all_to_all | solution.py:189

commit v3 on v2

--- a/solution.py
+++ b/solution.py
@@ -12,7 +12,7 @@
 BLOCK = 128
 PARTS = 8
 STRIP = 16
-UNROLL = 2
+UNROLL = 24
 DEAD = 1e30
 
 F32 = jnp.float32
@@ -71,10 +71,11 @@
     return jnp.concatenate([above, *parts], axis=0).T.astype(BF16)
 
 
-def pair_shares(group_no, slot, ids, catalog, strips, viewer, groups, duals):
+def pair_scores(index, work, catalog, strips, viewers_t, turned):
     features = catalog.shape[1] - PARTS
     last = catalog.shape[0] - 1
-    first, second = ids[group_no, slot], ids[group_no, slot + 1]
+    group_no, first, second = (work[row, index] for row in range(3))
+    viewer = viewers_t[pl.ds(pl.multiple_of(group_no * GROUP, GROUP), GROUP), :]
     vectors = jnp.concatenate(
         [
             catalog[jnp.minimum(first, last), :features, :],
@@ -83,16 +84,28 @@
         axis=1,
     )
     rows = [vectors, jnp.concatenate([strips[first], strips[second]], axis=1)]
-    if duals:
+    if turned is None:
+        viewer = viewer[:, : features + STRIP]
+    else:
+        viewer = viewer + turned
+        groups = (viewers_t.shape[1] - features - STRIP) // 3
         place = lax.broadcasted_iota(jnp.int32, (groups, 2 * BLOCK), 0)
         rows += [jnp.where(place == group_no, -1.0, 0.0).astype(BF16)] * 3
     scores = jnp.dot(viewer, jnp.concatenate(rows, axis=0), preferred_element_type=F32)
-    return jnp.clip(scores, 0.0, 1.0), vectors, first, second
-
-
-def totals_kernel(first_pass, ids, catalog, viewers_t, *refs):
-    groups, slots = ids.shape
+    return scores, vectors, group_no, first, second
+
+
+def for_pairs(work, unroll, body):
+    def step(number, _):
+        body([number * unroll + offset for offset in range(unroll)])
+        return 0
+
+    lax.fori_loop(0, lax.div(work[3, 0] + (unroll - 1), unroll), step, 0)
+
+
+def totals_kernel(first_pass, work, catalog, viewers_t, *refs):
     features = catalog.shape[1] - PARTS
+    turned = None
     if first_pass:
         outlay_out, demand_out, rate, strips, outlay_acc, demand_acc = refs
         limits = catalog[:, features:, :].astype(F32)
@@ -106,27 +119,23 @@
         turned = turned_duals(duals[...], viewers_t.shape[1])
     outlay_acc[...] = jnp.zeros_like(outlay_acc)
     demand_acc[...] = jnp.zeros_like(demand_acc)
-    lane = lax.broadcasted_iota(jnp.int32, (GROUP, BLOCK), 1)
-
-    def step(group_no, _):
-        start = pl.multiple_of(group_no * GROUP, GROUP)
-        viewer = viewers_t[pl.ds(start, GROUP), :]
-        viewer = viewer[:, : features + STRIP] if first_pass else viewer + turned
-        by_viewer = jnp.zeros((GROUP, BLOCK), F32)
-        for slot in range(0, slots, 2):
-            shares, _, first, second = pair_shares(
-                group_no, slot, ids, catalog, strips, viewer, groups, not first_pass
-            )
-            by_viewer = by_viewer + (shares[:, :BLOCK] + shares[:, BLOCK:])
+
+    lane = lax.broadcasted_iota(jnp.int32, (GROUP, 128), 1)
+
+    def pairs(indices):
+        demand = demand_acc[...]
+        scored = [pair_scores(i, work, catalog, strips, viewers_t, turned) for i in indices]
+        for scores, _, group_no, first, second in scored:
+            shares = jnp.clip(scores, 0.0, 1.0)
+            total = jnp.sum(shares[:, :BLOCK] + shares[:, BLOCK:], axis=1, keepdims=True)
+            demand = demand + jnp.where(lane == group_no, total, 0.0)
             folded = jnp.sum(shares.reshape(GROUP // 8, 8, 2 * BLOCK), axis=0)
             outlay_acc[first] += folded[:, :BLOCK]
             outlay_acc[second] += folded[:, BLOCK:]
-        demand = jnp.sum(by_viewer, axis=1, keepdims=True)
-        demand_acc[...] = jnp.where(lane == group_no, demand, demand_acc[...])
-        return 0
-
-    lax.fori_loop(0, groups, step, 0, unroll=UNROLL)
-    demand_out[...] = demand_acc[...].T[:groups, :]
+        demand_acc[...] = demand
+
+    for_pairs(work, UNROLL, pairs)
+    demand_out[...] = demand_acc[...].T[: demand_out.shape[0], :]
     peers = outlay_out.shape[0]
     outlay = jnp.sum(outlay_acc[:peers], axis=1)
     for peer in range(peers):
@@ -134,10 +143,9 @@
 
 
 def adv_kernel(
-    ids, own, catalog, viewers_t, viewers, outlays, old_prices, rate, duals,
+    work, own, catalog, viewers_t, viewers, outlays, old_prices, rate, duals,
     adv_out, own_prices, duals_out, strips_out, adv_acc, prices,
 ):
-    groups, slots = ids.shape
     prices[...] = new_prices(outlays, old_prices, rate)
     own_prices[...] = prices[pl.ds(own[0], 1), :]
     duals_out[...] = duals[...]
@@ -145,48 +153,55 @@
     turned = turned_duals(duals[...], viewers_t.shape[1])
     adv_acc[...] = jnp.zeros_like(adv_acc)
 
-    def step(group_no, _):
-        start = pl.multiple_of(group_no * GROUP, GROUP)
-        viewer_t = viewers_t[pl.ds(start, GROUP), :] + turned
-        viewer = viewers[:, pl.ds(start, GROUP)]
-        for slot in range(0, slots, 2):
-            shares, _, first, second = pair_shares(
-                group_no, slot, ids, catalog, strips_out, viewer_t, groups, True
-            )
-            terms = jnp.dot(viewer, shares.astype(BF16), preferred_element_type=F32)
+    def pairs(indices):
+        scored = [pair_scores(i, work, catalog, strips_out, viewers_t, turned) for i in indices]
+        weighed = [jnp.clip(one[0], 0.0, 1.0).astype(BF16) for one in scored]
+        for weights, (_, _, group_no, first, second) in zip(weighed, scored):
+            viewer = viewers[:, pl.ds(pl.multiple_of(group_no * GROUP, GROUP), GROUP)]
+            terms = jnp.dot(viewer, weights, preferred_element_type=F32)
             adv_acc[first] += terms[:, :BLOCK]
             adv_acc[second] += terms[:, BLOCK:]
-        return 0
-
-    lax.fori_loop(0, groups, step, 0, unroll=UNROLL)
+
+    for_pairs(work, UNROLL, pairs)
     adv_out[...] = (adv_acc[: adv_out.shape[0]] * (1.0 / GROUP)).astype(BF16)
 
 
-def imp_kernel(ids, catalog, viewers_t, strips, duals, imp_out):
-    groups, slots = ids.shape
-    features = catalog.shape[1] - PARTS
+def imp_kernel(work, catalog, viewers_t, strips, duals, imp_out, imp_acc):
     turned = turned_duals(duals[...], viewers_t.shape[1])
-
-    def step(group_no, _):
-        start = pl.multiple_of(group_no * GROUP, GROUP)
-        viewer_t = viewers_t[pl.ds(start, GROUP), :] + turned
-        imp_part = jnp.zeros((features, GROUP), F32)
-        for slot in range(0, slots, 2):
-            shares, vectors, _, _ = pair_shares(
-                group_no, slot, ids, catalog, strips, viewer_t, groups, True
+    imp_acc[...] = jnp.zeros_like(imp_acc)
+
+    def pairs(indices):
+        scored = [pair_scores(i, work, catalog, strips, viewers_t, turned) for i in indices]
+        weighed = [jnp.clip(one[0], 0.0, 1.0).astype(BF16) for one in scored]
+        for weights, (_, vectors, group_no, _, _) in zip(weighed, scored):
+            imp_acc[group_no] += lax.dot_general(
+                vectors, weights, (((1,), (1,)), ((), ())), preferred_element_type=F32
             )
-            imp_part = imp_part + lax.dot_general(
-                vectors, shares.astype(BF16), (((1,), (1,)), ((), ())),
-                preferred_element_type=F32,
-            )
-        imp_out[lax.rem(group_no, 2), lax.div(group_no, 2)] = imp_part.astype(BF16)
-        return 0
-
-    lax.fori_loop(0, groups, step, 0, unroll=UNROLL)
+
+    for_pairs(work, UNROLL, pairs)
+    for group_no in range(imp_acc.shape[0]):
+        imp_out[group_no % 2, group_no // 2] = imp_acc[group_no].astype(BF16)
 
 
 def to_all(value, axis):
     return lax.all_to_all(value, axis, 0, 0, tiled=True)
+
+
+def work_list(ids, counts, dead):
+    _, slots = ids.shape
+    ids = jnp.where(jnp.arange(slots)[None, :] < counts, ids, dead)
+    live = (jnp.arange(0, slots, 2)[None, :] < counts).reshape(-1)
+    pairs = jnp.arange(live.size)
+    entries = jnp.arange(-(-live.size // UNROLL) * UNROLL)
+    place = jnp.sum(live[None, :] & (pairs[None, :] < pairs[:, None]), axis=1)
+    chosen = live[None, :] & (place[None, :] == entries[:, None])
+    group_no = pairs // (slots // 2)
+    rows = [
+        jnp.sum(jnp.where(chosen, row[None, :] - rest, 0), axis=1) + rest
+        for row, rest in ((group_no, 0), (ids[:, ::2].reshape(-1), dead), (ids[:, 1::2].reshape(-1), dead))
+    ]
+    rows.append(jnp.full_like(entries, jnp.sum(live)))
+    return jnp.stack(rows).astype(jnp.int32)
 
 
 def call(kernel, n_smem, out_shape, scratch, *args):
@@ -204,8 +219,7 @@
     features = impression_vectors.shape[0]
     groups, _, slots = blocks.shape
     n_imp, n_adv = lax.axis_size(IMP), lax.axis_size(ADV)
-    live = jnp.arange(slots)[None, :] < counts
-    ids = jnp.where(live, blocks.reshape(groups, slots) // n_adv, n_imp)
+    work = work_list(blocks.reshape(groups, slots) // n_adv, counts, n_imp)
     own = lax.axis_index(IMP).astype(jnp.int32).reshape(1)
     caps = capacity.reshape(groups, GROUP)
     ones = jnp.ones((3, impression_vectors.shape[1]), BF16)
@@ -222,11 +236,11 @@
     exchange = [((n_imp, n_imp, BLOCK), F32), ((groups, GROUP), F32)]
     levels = [((n_imp, BLOCK), F32)]
     strips = [((n_imp + 1, STRIP, BLOCK), BF16)]
-    sums = [((n_imp + 1, 8, BLOCK), F32), ((GROUP, BLOCK), F32)]
+    sums = [((n_imp + 1, 8, BLOCK), F32), ((GROUP, 128), F32)]
 
     outlays, demand, rate = call(
         functools.partial(totals_kernel, True), 1, exchange + levels, strips + sums,
-        ids, catalog, viewers_t,
+        work, catalog, viewers_t,
     )
     prices = jnp.zeros((n_imp, BLOCK), F32)
     duals = jnp.zeros((groups, GROUP), F32)
@@ -243,7 +257,7 @@
         outlays, demand, prices = call(
             functools.partial(totals_kernel, False), 1, exchange + levels,
             strips + sums,
-            ids, catalog, viewers_t, outlays, prices, rate, duals,
+            work, catalog, viewers_t, outlays, prices, rate, duals,
         )
     outlays, duals = meet(outlays, demand, duals)
     adv_parts, own_prices, out_duals, strip_rows = call(
@@ -255,12 +269,13 @@
             *strips,
         ],
         [((n_imp + 1, features, BLOCK), F32)] + levels,
-        ids, own, catalog, viewers_t, impression_vectors, outlays, prices, rate, duals,
+        work, own, catalog, viewers_t, impression_vectors, outlays, prices, rate, duals,
     )
     adv_parts = to_all(adv_parts, IMP)
     (imp_parts,) = call(
-        imp_kernel, 1, [((2, groups // 2, features, GROUP), BF16)], [],
-        ids, catalog, viewers_t, strip_rows, duals,
+        imp_kernel, 1, [((2, groups // 2, features, GROUP), BF16)],
+        [((groups, features, GROUP), F32)],
+        work, catalog, viewers_t, strip_rows, duals,
     )
     core = lax.axis_index("core")
     kept = lax.dynamic_index_in_dim(imp_parts, core, 0, keepdims=False)

time: 192 us -> 173 us (0.901)
  Pallas kernels: 34.7 us -> 16 us
    pallas_call x6, Pallas kernels: 34.7 us -> 16 us  [call(): pl.pallas_call(kernel, in_specs=[SMEM] * n_smem + [VMEM] * (len(args) - n...]
  transfers between devices with their start and end apart: 6 -> 6, of which waited for: 3 -> 3; matrix products, arithmetic and copies ran while one was open for 1% -> 2% of each run, Pallas kernels for 0% -> 0%
where the time goes in v3:
time: 173 us; the launch traced here: 172 us
  blocking collectives  67.7 us (39%)
  starting transfers between devices  50.4 us (29%)
  waiting for transfers between devices  30.7 us (18%)
  Pallas kernels  16 us (9%)
  local copies, waits for them, and re-layouts  3.67 us (2%)
  other arithmetic  2.7 us (2%)
    psum x3, blocking collectives, meet(): lax.psum((pair[0] + pair[1]).reshape(-1), 'y').reshape(demand.shape)  48.7 us
    all_to_all x5, starting transfers between devices, to_all(): return lax.all_to_all(value, axis, 0, 0, tiled=True)  48.5 us
    all_to_all x5, waiting for transfers between devices, to_all(): return lax.all_to_all(value, axis, 0, 0, tiled=True)  29.4 us
    pallas_call x6, Pallas kernels, call(): pl.pallas_call(kernel, in_specs=[SMEM] * n_smem + [VMEM] * (len(args) - n...  16 us
    all_to_all x1, blocking collectives, to_all(): return lax.all_to_all(value, axis, 0, 0, tiled=True)  13.5 us
    all_gather x3, blocking collectives, meet(): pair = lax.all_gather(demand, 'core', axis=0)  5.46 us
  transfers between devices with their start and end apart: 6, of which 3 were waited for; matrix products, arithmetic and copies ran while one was open for 2% of the time, Pallas kernels for 0%

profile of v3, /device:TPU:2, one launch (start us, length us, event | category | flops | bytes accessed | tf_op | source)
XLA Modules:
  0.0 172.0 jit_solution(9257465544408429676)
XLA Ops:
  0.6 0.0 copy-start.2
  0.6 0.6 copy-done.2
  1.3 0.0 copy-start.1
  1.3 0.7 copy-done.1
  2.0 0.9 shard_map.93
  2.9 0.0 copy-start.4
  2.9 0.0 copy-start
  2.9 13.6 %all-to-all-start = ((bf16[32,72,128]{2,1,0:T(8,128)(2,1)}), bf16[32,72,128]{2,1,0:T(8,128)(2,1)S(1)}, u32[]{:S(2)}, u32[]{:S(2)}) async-start(bf16[32,72,128]{2,1,0:T(8,128)(2,1)} %shard_map.93), calls=%async_computation | async-start | bytes 1179648 | tf_op jit(solution)/shard_map/all_to_all | solution.py:187
  16.5 0.0 copy-start.5
  16.5 0.0 copy-done.4
  16.5 0.6 copy-done.5
  17.2 0.1 broadcast_compare_fusion
  17.3 0.7 convert_reduce_fusion.1
  18.0 0.1 lt.61
  18.1 0.1 copy.16
  18.2 0.1 sub.37
  18.3 0.1 copy.17
  18.4 0.1 sub.39
  18.5 0.0 copy-done
  18.5 0.3 copy.18
  18.8 0.1 pad.1.clone
  18.9 0.1 pad.2.clone
  18.9 0.7 pad.6.clone
  19.6 0.1 convert_reduce_fusion
  19.8 0.1 select_reduce_fusion.2
  19.9 0.1 add_add_fusion.work
  20.0 0.2 maximum_bitcast_fusion.viewers_t
  20.2 14.6 %all-to-all-done.catalog = bf16[32,72,128]{2,1,0:T(8,128)(2,1)S(1)} async-done(((bf16[32,72,128]{2,1,0:T(8,128)(2,1)}), bf16[32,72,128]{2,1,0:T(8,128)(2,1)S(1)}, u32[]{:S(2)}, u32[]{:S(2)}) %all-to-all-start) | async-done | bytes 589856 | tf_op jit(solution)/shard_map/all_to_all | solution.py:187
  34.7 2.8 %shard_map.94 = (f32[32,32,128]{2,1,0:T(8,128)}, f32[16,128]{1,0:T(8,128)S(1)}, f32[32,128]{1,0:T(8,128)S(1)}) custom-call(s32[4,72]{1,0:T(4,128)S(1)} %add_add_fusion.work, bf16[32,72,128]{2,1,0:T(8,128)(2,1)S(1)} %all-to-all-done.catalog, bf16[2048,128]{1,0:T(8,128)(2,1)S(1)} %maximum_bitcast_fusion.viewers_t), custom_call_target="tpu_custom_call" | custom-call | tf_op jit(solution)/shard_map/pallas_call | solution.py:208
  37.6 5.6 %all-to-all-start.1 = ((f32[32,32,128]{2,1,0:T(8,128)}), f32[32,32,128]{2,1,0:T(8,128)S(1)}, u32[]{:S(2)}, u32[]{:S(2)}) async-start(f32[32,32,128]{2,1,0:T(8,128)} %get-tuple-element.17), calls=%async_computation.1 | async-start | bytes 1048576 | tf_op jit(solution)/shard_map/all_to_all | solution.py:187
  43.1 1.8 %all-gather = f32[32,128]{1,0:T(8,128)S(1)} all-gather(f32[16,128]{1,0:T(8,128)S(1)} %get-tuple-element.19), channel_id=2, replica_groups=mesh['z'=8,'x'=4,'y'=8,'core'=2] {'core'}, dimensions={0}, use_global_device_ids=true | all-gather | bytes 24576 | tf_op jit(solution)/shard_map/all_gather | solution.py:250
  45.0 0.0 copy-start.3
  45.0 17.9 %psum.21 = f32[2048]{0:T(1024)S(1)} all-reduce(f32[2048]{0:T(1024)S(1)} %fusion.5), channel_id=1, replica_groups=mesh['z'=8,'x'=4,'y'=8,'core'=2] {'y'}, use_global_device_ids=true, to_apply=%region_5.6 | all-reduce | flops 2048 | bytes 16384 | tf_op jit(solution)/shard_map/psum | solution.py:251
  62.8 0.0 copy-done.3
  62.9 0.0 all-to-all-done.1.refs_0_
  62.9 3.0 %shard_map.95 = (f32[32,32,128]{2,1,0:T(8,128)}, f32[16,128]{1,0:T(8,128)S(1)}, f32[32,128]{1,0:T(8,128)S(1)}) custom-call(s32[4,72]{1,0:T(4,128)S(1)} %add_add_fusion.work, bf16[32,72,128]{2,1,0:T(8,128)(2,1)S(1)} %all-to-all-done.catalog, bf16[2048,128]{1,0:T(8,128)(2,1)S(1)} %maximum_bitcast_fusion.viewers_t, f32[32,32,128]{2,1,0:T(8,128)S(1)} %all-to-all-done.1.refs_0_, ...), custom_call_target="tpu_custom_call" | custom-call | tf_op jit(solution)/shard_map/pallas_call | solution.py:208
  65.9 9.8 %all-to-all-start.2 = ((f32[32,32,128]{2,1,0:T(8,128)}), f32[32,32,128]{2,1,0:T(8,128)S(1)}, u32[]{:S(2)}, u32[]{:S(2)}) async-start(f32[32,32,128]{2,1,0:T(8,128)} %get-tuple-element.20), calls=%async_computation.2 | async-start | bytes 1048576 | tf_op jit(solution)/shard_map/all_to_all | solution.py:187
  75.6 1.8 %all-gather.1 = f32[32,128]{1,0:T(8,128)S(1)} all-gather(f32[16,128]{1,0:T(8,128)S(1)} %get-tuple-element.22), channel_id=3, replica_groups=mesh['z'=8,'x'=4,'y'=8,'core'=2] {'core'}, dimensions={0}, use_global_device_ids=true | all-gather | bytes 24576 | tf_op jit(solution)/shard_map/all_gather | solution.py:250
  77.5 15.2 %psum.22 = f32[2048]{0:T(1024)S(1)} all-reduce(f32[2048]{0:T(1024)S(1)} %fusion.4), channel_id=1, replica_groups=mesh['z'=8,'x'=4,'y'=8,'core'=2] {'y'}, use_global_device_ids=true, to_apply=%region_6.7 | all-reduce | flops 2048 | bytes 16384 | tf_op jit(solution)/shard_map/psum | solution.py:251
  92.7 0.0 all-to-all-done.2.refs_0_
  92.7 3.0 %shard_map.96 = (f32[32,32,128]{2,1,0:T(8,128)}, f32[16,128]{1,0:T(8,128)S(1)}, f32[32,128]{1,0:T(8,128)S(1)}) custom-call(s32[4,72]{1,0:T(4,128)S(1)} %add_add_fusion.work, bf16[32,72,128]{2,1,0:T(8,128)(2,1)S(1)} %all-to-all-done.catalog, bf16[2048,128]{1,0:T(8,128)(2,1)S(1)} %maximum_bitcast_fusion.viewers_t, f32[32,32,128]{2,1,0:T(8,128)S(1)} %all-to-all-done.2.refs_0_, ...), custom_call_target="tpu_custom_call" | custom-call | tf_op jit(solution)/shard_map/pallas_call | solution.py:208
  95.7 9.8 %all-to-all-start.3 = ((f32[32,32,128]{2,1,0:T(8,128)}), f32[32,32,128]{2,1,0:T(8,128)S(1)}, u32[]{:S(2)}, u32[]{:S(2)}) async-start(f32[32,32,128]{2,1,0:T(8,128)} %get-tuple-element.23), calls=%async_computation.3 | async-start | bytes 1048576 | tf_op jit(solution)/shard_map/all_to_all | solution.py:187
  105.5 1.8 %all-gather.2 = f32[32,128]{1,0:T(8,128)S(1)} all-gather(f32[16,128]{1,0:T(8,128)S(1)} %get-tuple-element.25), channel_id=4, replica_groups=mesh['z'=8,'x'=4,'y'=8,'core'=2] {'core'}, dimensions={0}, use_global_device_ids=true | all-gather | bytes 24576 | tf_op jit(solution)/shard_map/all_gather | solution.py:250
  107.3 15.6 %psum.23 = f32[2048]{0:T(1024)S(1)} all-reduce(f32[2048]{0:T(1024)S(1)} %fusion.3), channel_id=1, replica_groups=mesh['z'=8,'x'=4,'y'=8,'core'=2] {'y'}, use_global_device_ids=true, to_apply=%region_7.8 | all-reduce | flops 2048 | bytes 16384 | tf_op jit(solution)/shard_map/psum | solution.py:251
  122.9 0.0 all-to-all-done.3.outlays
  122.9 3.4 %shard_map.97 = (bf16[32,64,128]{2,1,0:T(8,128)(2,1)}, f32[1,128]{1,0:T(1,128)}, f32[16,128]{1,0:T(8,128)}, bf16[33,16,128]{2,1,0:T(8,128)(2,1)S(1)}) custom-call(s32[4,72]{1,0:T(4,128)S(1)} %add_add_fusion.work, s32[1]{0:T(128)} %bitcast.5.own, bf16[32,72,128]{2,1,0:T(8,128)(2,1)S(1)} %all-to-all-done.catalog, ...), custom_call_target="tpu_custom_call" | custom-call | tf_op jit(solution)/shard_map/pallas_call | solution.py:208
  126.4 2.9 %shard_map.98 = bf16[2,8,64,128]{3,2,1,0:T(8,128)(2,1)S(1)} custom-call(s32[4,72]{1,0:T(4,128)S(1)} %add_add_fusion.work, bf16[32,72,128]{2,1,0:T(8,128)(2,1)S(1)} %all-to-all-done.catalog, bf16[2048,128]{1,0:T(8,128)(2,1)S(1)} %maximum_bitcast_fusion.viewers_t, bf16[33,16,128]{2,1,0:T(8,128)(2,1)S(1)} %get-tuple-element.28.strips, f32[16,128]{1,0:T(8,128)S(1)} %fusion.7.duals), custom_call_target="tpu_custom_call" | custom-call | tf_op jit(solution)/shard_map/pallas_call | solution.py:208
  129.3 1.9 %collective-permute-start = (bf16[8,64,128]{2,1,0:T(8,128)(2,1)S(1)}, bf16[8,64,128]{2,1,0:T(8,128)(2,1)S(1)}, u32[]{:S(2)}, u32[]{:S(2)}) collective-permute-start(bf16[8,64,128]{2,1,0:T(8,128)(2,1)S(1)} %dynamic-slice_bitcast_fusion), channel_id=1, source_target_pairs={{0,1},{1,0},{2,3},{3,2},{4,5},{5,4},{6,7},{7,6},{8,9},{9,8},{10,11... | collective-permute-start | bytes 393224 | tf_op jit(solution)/shard_map/ppermute | solution.py:283
  131.2 1.3 collective-permute-done
  132.6 13.5 %all_to_all.30 = bf16[8,64,128]{2,1,0:T(8,128)(2,1)S(1)} all-to-all(bf16[8,64,128]{2,1,0:T(8,128)(2,1)S(1)} %fusion), channel_id=1, replica_groups=mesh['z'=8,'x'=4,'y'=8,'core'=2] {'y'}, dimensions={0} | all-to-all | bytes 262144 | tf_op jit(solution)/shard_map/all_to_all | solution.py:187
  146.1 9.8 %all-to-all-start.5 = ((bf16[32,64,128]{2,1,0:T(8,128)(2,1)}), bf16[32,64,128]{2,1,0:T(8,128)(2,1)S(1)}, u32[]{:S(2)}, u32[]{:S(2)}) async-start(bf16[32,64,128]{2,1,0:T(8,128)(2,1)} %get-tuple-element.29), calls=%async_computation.5 | async-start | bytes 1048576 | tf_op jit(solution)/shard_map/all_to_all | solution.py:187
  155.9 0.6 reduce_sum.74
  156.5 14.8 %all-to-all-done.5 = bf16[32,64,128]{2,1,0:T(8,128)(2,1)S(1)} async-done(((bf16[32,64,128]{2,1,0:T(8,128)(2,1)}), bf16[32,64,128]{2,1,0:T(8,128)(2,1)S(1)}, u32[]{:S(2)}, u32[]{:S(2)}) %all-to-all-start.5) | async-done | bytes 524320 | tf_op jit(solution)/shard_map/all_to_all | solution.py:187
  171.3 0.7 reduce_sum.75
  (19 shorter events, 0.2 us)
Async XLA Ops:
  0.6 0.7 copy-start.2
  1.3 0.7 copy-start.1
  2.9 13.6 %copy-start.4 = (s32[16,1,8]{0,2,1:T(8,128)S(1)}, s32[16,1,8]{0,2,1:T(8,128)}, u32[]{:S(2)}) copy-start(s32[16,1,8]{0,2,1:T(8,128)} %param.10) | copy-start | bytes 1540
  2.9 15.6 %copy-start = (bf16[64,2048]{1,0:T(8,128)(2,1)S(1)}, bf16[64,2048]{1,0:T(8,128)(2,1)}, u32[]{:S(2)}) copy-start(bf16[64,2048]{1,0:T(8,128)(2,1)} %viewers.1) | copy-start | bytes 786436
  2.9 31.8 %all-to-all-start = ((bf16[32,72,128]{2,1,0:T(8,128)(2,1)}), bf16[32,72,128]{2,1,0:T(8,128)(2,1)S(1)}, u32[]{:S(2)}, u32[]{:S(2)}) async-start(bf16[32,72,128]{2,1,0:T(8,128)(2,1)} %shard_map.93), calls=%async_computation | async-start | bytes 1179648 | tf_op jit(solution)/shard_map/all_to_all | solution.py:187
  16.5 0.7 copy-start.5
  37.6 25.3 %all-to-all-start.1 = ((f32[32,32,128]{2,1,0:T(8,128)}), f32[32,32,128]{2,1,0:T(8,128)S(1)}, u32[]{:S(2)}, u32[]{:S(2)}) async-start(f32[32,32,128]{2,1,0:T(8,128)} %get-tuple-element.17), calls=%async_computation.1 | async-start | bytes 1048576 | tf_op jit(solution)/shard_map/all_to_all | solution.py:187
  45.0 17.9 %copy-start.3 = (f32[2048]{0:T(1024)S(1)}, f32[2048]{0:T(1024)}, u32[]{:S(2)}) copy-start(f32[2048]{0:T(1024)} %param.9) | copy-start | bytes 24580
  65.9 26.9 %all-to-all-start.2 = ((f32[32,32,128]{2,1,0:T(8,128)}), f32[32,32,128]{2,1,0:T(8,128)S(1)}, u32[]{:S(2)}, u32[]{:S(2)}) async-start(f32[32,32,128]{2,1,0:T(8,128)} %get-tuple-element.20), calls=%async_computation.2 | async-start | bytes 1048576 | tf_op jit(solution)/shard_map/all_to_all | solution.py:187
  95.7 27.2 %all-to-all-start.3 = ((f32[32,32,128]{2,1,0:T(8,128)}), f32[32,32,128]{2,1,0:T(8,128)S(1)}, u32[]{:S(2)}, u32[]{:S(2)}) async-start(f32[32,32,128]{2,1,0:T(8,128)} %get-tuple-element.23), calls=%async_computation.3 | async-start | bytes 1048576 | tf_op jit(solution)/shard_map/all_to_all | solution.py:187
  129.3 3.2 %collective-permute-start = (bf16[8,64,128]{2,1,0:T(8,128)(2,1)S(1)}, bf16[8,64,128]{2,1,0:T(8,128)(2,1)S(1)}, u32[]{:S(2)}, u32[]{:S(2)}) collective-permute-start(bf16[8,64,128]{2,1,0:T(8,128)(2,1)S(1)} %dynamic-slice_bitcast_fusion), channel_id=1, source_target_pairs={{0,1},{1,0},{2,3},{3,2},{4,5},{5,4},{6,7},{7,6},{8,9},{9,8},{10,11... | collective-permute-start | bytes 393224 | tf_op jit(solution)/shard_map/ppermute | solution.py:283
  146.1 25.2 %all-to-all-start.5 = ((bf16[32,64,128]{2,1,0:T(8,128)(2,1)}), bf16[32,64,128]{2,1,0:T(8,128)(2,1)S(1)}, u32[]{:S(2)}, u32[]{:S(2)}) async-start(bf16[32,64,128]{2,1,0:T(8,128)(2,1)} %get-tuple-element.29), calls=%async_computation.5 | async-start | bytes 1048576 | tf_op jit(solution)/shard_map/all_to_all | solution.py:187

commit v4 on v3

--- a/solution.py
+++ b/solution.py
@@ -18,7 +18,7 @@
 F32 = jnp.float32
 BF16 = jnp.bfloat16
 IMP = ("z", "x")
-ADV = ("y", "core")
+ADV = "adv"
 VMEM = pl.BlockSpec(memory_space=pltpu.VMEM)
 SMEM = pl.BlockSpec(memory_space=pltpu.SMEM)
 PARAMS = pltpu.CompilerParams(vmem_limit_bytes=16 << 20)
@@ -180,7 +180,20 @@
 
     for_pairs(work, UNROLL, pairs)
     for group_no in range(imp_acc.shape[0]):
-        imp_out[group_no % 2, group_no // 2] = imp_acc[group_no].astype(BF16)
+        imp_out[ring_of(group_no), group_no // 2] = imp_acc[group_no]
+
+
+def chip_groups():
+    return [[a, a + 1] for a in range(0, lax.axis_size(ADV), 2)]
+
+
+def ring_of(place):
+    return (place // 2 + place + 1) % 2
+
+
+def ring_groups():
+    places = range(lax.axis_size(ADV))
+    return [[place for place in places if ring_of(place) == ring] for ring in (0, 1)]
 
 
 def to_all(value, axis):
@@ -204,14 +217,14 @@
     return jnp.stack(rows).astype(jnp.int32)
 
 
-def call(kernel, n_smem, out_shape, scratch, *args):
+def call(kernel, n_smem, out_shape, scratch, *args, params=PARAMS):
     return pl.pallas_call(
         kernel,
         in_specs=[SMEM] * n_smem + [VMEM] * (len(args) - n_smem),
         out_specs=(VMEM,) * len(out_shape),
         out_shape=tuple(jax.ShapeDtypeStruct(shape, dtype) for shape, dtype in out_shape),
         scratch_shapes=[pltpu.VMEM(shape, dtype) for shape, dtype in scratch],
-        compiler_params=PARAMS,
+        compiler_params=params,
     )(*args)
 
 
@@ -229,7 +242,7 @@
 
     (packed,) = call(
         pack_kernel, 0, [((n_imp, features + PARTS, BLOCK), BF16)], [],
-        advertiser_vectors, spend_limits.reshape(1, BLOCK),
+        advertiser_vectors, spend_limits.reshape(1, BLOCK), params=None,
     )
     catalog = to_all(packed, IMP)
 
@@ -247,8 +260,10 @@
 
     def meet(outlays, demand, duals):
         outlays = to_all(outlays, IMP)
-        pair = lax.all_gather(demand, "core", axis=0)
-        demand = lax.psum((pair[0] + pair[1]).reshape(-1), "y").reshape(demand.shape)
+        pair = lax.all_gather(demand, ADV, axis=0, axis_index_groups=chip_groups())
+        demand = lax.psum(
+            (pair[0] + pair[1]).reshape(-1), ADV, axis_index_groups=ring_groups()
+        ).reshape(demand.shape)
         duals = jnp.maximum(duals + demand / caps - 1.0, 0.0)
         return outlays, duals
 
@@ -273,16 +288,16 @@
     )
     adv_parts = to_all(adv_parts, IMP)
     (imp_parts,) = call(
-        imp_kernel, 1, [((2, groups // 2, features, GROUP), BF16)],
+        imp_kernel, 1, [((2, groups // 2, features, GROUP), F32)],
         [((groups, features, GROUP), F32)],
         work, catalog, viewers_t, strip_rows, duals,
     )
-    core = lax.axis_index("core")
-    kept = lax.dynamic_index_in_dim(imp_parts, core, 0, keepdims=False)
-    given = lax.dynamic_index_in_dim(imp_parts, 1 - core, 0, keepdims=False)
-    given = lax.ppermute(given, "core", [(0, 1), (1, 0)])
-    imp_parts = (kept.astype(F32) + given.astype(F32)).astype(BF16)
-    imp_parts = to_all(imp_parts, "y")
+    ring = ring_of(lax.axis_index(ADV))
+    kept = lax.dynamic_index_in_dim(imp_parts, ring, 0, keepdims=False)
+    given = lax.dynamic_index_in_dim(imp_parts, 1 - ring, 0, keepdims=False)
+    given = lax.ppermute(given, ADV, [(a, a ^ 1) for a in range(n_adv)])
+    imp_parts = (kept + given).astype(BF16)
+    imp_parts = lax.all_to_all(imp_parts, ADV, 0, 0, tiled=True, axis_index_groups=ring_groups())
     impression_grad = jnp.sum(imp_parts.astype(F32), axis=0).astype(BF16)
     advertiser_grad = jnp.sum(adv_parts.astype(F32), axis=0).astype(BF16)
     return own_prices.reshape(-1), out_duals.reshape(-1), impression_grad, advertiser_grad
@@ -290,18 +305,18 @@
 
 def solution(mesh):
     n_imp, n_adv = (mesh.shape[axis] for axis in ("imp", "adv"))
-    chips = jax.sharding.Mesh(mesh.devices.reshape(n_imp // 4, 4, n_adv // 2, 2), IMP + ADV)
+    chips = jax.sharding.Mesh(mesh.devices.reshape(n_imp // 4, 4, n_adv), IMP + (ADV,))
     return jax.shard_map(
         local,
         mesh=chips,
         in_specs=(
             P(None, IMP),
-            P(None, IMP + ADV),
-            P(IMP + ADV),
+            P(None, IMP + (ADV,)),
+            P(IMP + (ADV,)),
             P(IMP),
             P(IMP, ADV, None),
             P(IMP, ADV),
         ),
-        out_specs=(P(IMP + ADV), P(IMP), P(None, IMP + ADV), P(None, IMP + ADV)),
+        out_specs=(P(IMP + (ADV,)), P(IMP), P(None, IMP + (ADV,)), P(None, IMP + (ADV,))),
         check_vma=False,
     )

time: 173 us -> 169 us (0.977)
  the two profiles are of different devices: /device:TPU:2 before, /device:TPU:8 now
where the time goes in v4:
time: 169 us; the launch traced here: 168 us
  blocking collectives  63 us (37%)
  starting transfers between devices  44.5 us (26%)
  waiting for transfers between devices  38.2 us (23%)
  Pallas kernels  16.6 us (10%)
  other arithmetic  2.7 us (2%)
  local copies, waits for them, and re-layouts  2.32 us (1%)
    psum x3, blocking collectives, meet(): lax.psum((pair[0] + pair[1]).reshape(-1), ADV, axis_index_groups=ring_gro...  43.8 us
    all_to_all x5, starting transfers between devices, to_all(): return lax.all_to_all(value, axis, 0, 0, tiled=True)  42.6 us
    all_to_all x5, waiting for transfers between devices, to_all(): return lax.all_to_all(value, axis, 0, 0, tiled=True)  36.7 us
    pallas_call x6, Pallas kernels, call(): pl.pallas_call(kernel, in_specs=[SMEM] * n_smem + [VMEM] * (len(args) - n...  16.6 us
    all_to_all x1, blocking collectives, local(): lax.all_to_all(imp_parts, ADV, 0, 0, tiled=True, axis_index_groups=ring_g...  13.7 us
    all_gather x3, blocking collectives, meet(): pair = lax.all_gather(demand, ADV, axis=0, axis_index_groups=chip_groups())  5.46 us
  transfers between devices with their start and end apart: 6, of which 6 were waited for; matrix products, arithmetic and copies ran while one was open for 2% of the time, Pallas kernels for 0%

profile of v4, /device:TPU:8, one launch (start us, length us, event | category | flops | bytes accessed | tf_op | source)
XLA Modules:
  0.0 168.2 jit_solution(9645290952561215334)
XLA Ops:
  0.6 1.6 shard_map.93
  2.2 0.0 copy-start
  2.2 13.3 %all-to-all-start = ((bf16[32,72,128]{2,1,0:T(8,128)(2,1)}), bf16[32,72,128]{2,1,0:T(8,128)(2,1)S(1)}, u32[]{:S(2)}, u32[]{:S(2)}) async-start(bf16[32,72,128]{2,1,0:T(8,128)(2,1)} %shard_map.93), calls=%async_computation | async-start | bytes 1179648 | tf_op jit(solution)/shard_map/all_to_all | solution.py:200
  15.5 0.0 copy-start.2
  15.6 0.0 copy-start.3
  15.6 0.6 copy-done.2
  16.2 0.0 copy-done.3
  16.3 0.1 broadcast_compare_fusion
  16.4 0.7 convert_reduce_fusion.1
  17.1 0.1 lt.67
  17.2 0.1 copy.17
  17.3 0.1 sub.43
  17.4 0.1 copy.16
  17.4 0.1 sub.41
  17.5 0.0 copy-done
  17.5 0.3 copy.18
  17.8 0.1 pad.2.clone
  17.9 0.1 pad.1.clone
  18.0 0.7 pad.6.clone
  18.7 0.1 convert_reduce_fusion
  18.8 0.1 select_reduce_fusion.2
  19.0 0.1 add_add_fusion.work
  19.0 0.2 maximum_bitcast_fusion.viewers_t
  19.2 15.3 %all-to-all-done.catalog = bf16[32,72,128]{2,1,0:T(8,128)(2,1)S(1)} async-done(((bf16[32,72,128]{2,1,0:T(8,128)(2,1)}), bf16[32,72,128]{2,1,0:T(8,128)(2,1)S(1)}, u32[]{:S(2)}, u32[]{:S(2)}) %all-to-all-start) | async-done | bytes 589856 | tf_op jit(solution)/shard_map/all_to_all | solution.py:200
  34.5 2.8 %shard_map.94 = (f32[32,32,128]{2,1,0:T(8,128)}, f32[16,128]{1,0:T(8,128)S(1)}, f32[32,128]{1,0:T(8,128)S(1)}) custom-call(s32[4,72]{1,0:T(4,128)S(1)} %add_add_fusion.work, bf16[32,72,128]{2,1,0:T(8,128)(2,1)S(1)} %all-to-all-done.catalog, bf16[2048,128]{1,0:T(8,128)(2,1)S(1)} %maximum_bitcast_fusion.viewers_t), custom_call_target="tpu_custom_call" | custom-call | tf_op jit(solution)/shard_map/pallas_call | solution.py:221
  37.4 4.8 %all-to-all-start.1 = ((f32[32,32,128]{2,1,0:T(8,128)}), f32[32,32,128]{2,1,0:T(8,128)S(1)}, u32[]{:S(2)}, u32[]{:S(2)}) async-start(f32[32,32,128]{2,1,0:T(8,128)} %get-tuple-element.17), calls=%async_computation.1 | async-start | bytes 1048576 | tf_op jit(solution)/shard_map/all_to_all | solution.py:200
  42.2 1.8 %all-gather = f32[32,128]{1,0:T(8,128)S(1)} all-gather(f32[16,128]{1,0:T(8,128)S(1)} %get-tuple-element.19), channel_id=2, replica_groups={{0,1},{2,3},{4,5},{6,7},{8,9},{10,11},{12,13},{14,15},{16,17},{18,19},{..., dimensions={0}, use_global_device_ids=true | all-gather | bytes 24576 | tf_op jit(solution)/shard_map/all_gather | solution.py:263
  44.0 0.0 copy-start.1
  44.0 15.0 %psum.21 = f32[2048]{0:T(1024)S(1)} all-reduce(f32[2048]{0:T(1024)S(1)} %fusion.5), channel_id=1, replica_groups={{1,2,5,6,9,10,13,14},{0,3,4,7,8,11,12,15},{17,18,21,22,25,26,29,30},{16..., use_global_device_ids=true, to_apply=%region_5.6 | all-reduce | flops 2048 | bytes 16384 | tf_op jit(solution)/shard_map/psum | solution.py:264
  59.1 0.0 copy-done.1
  59.1 0.1 all-to-all-done.1.refs_0_
  59.2 3.0 %shard_map.95 = (f32[32,32,128]{2,1,0:T(8,128)}, f32[16,128]{1,0:T(8,128)S(1)}, f32[32,128]{1,0:T(8,128)S(1)}) custom-call(s32[4,72]{1,0:T(4,128)S(1)} %add_add_fusion.work, bf16[32,72,128]{2,1,0:T(8,128)(2,1)S(1)} %all-to-all-done.catalog, bf16[2048,128]{1,0:T(8,128)(2,1)S(1)} %maximum_bitcast_fusion.viewers_t, f32[32,32,128]{2,1,0:T(8,128)S(1)} %all-to-all-done.1.refs_0_, ...), custom_call_target="tpu_custom_call" | custom-call | tf_op jit(solution)/shard_map/pallas_call | solution.py:221
  62.1 9.4 %all-to-all-start.2 = ((f32[32,32,128]{2,1,0:T(8,128)}), f32[32,32,128]{2,1,0:T(8,128)S(1)}, u32[]{:S(2)}, u32[]{:S(2)}) async-start(f32[32,32,128]{2,1,0:T(8,128)} %get-tuple-element.20), calls=%async_computation.2 | async-start | bytes 1048576 | tf_op jit(solution)/shard_map/all_to_all | solution.py:200
  71.5 1.8 %all-gather.1 = f32[32,128]{1,0:T(8,128)S(1)} all-gather(f32[16,128]{1,0:T(8,128)S(1)} %get-tuple-element.22), channel_id=3, replica_groups={{0,1},{2,3},{4,5},{6,7},{8,9},{10,11},{12,13},{14,15},{16,17},{18,19},{..., dimensions={0}, use_global_device_ids=true | all-gather | bytes 24576 | tf_op jit(solution)/shard_map/all_gather | solution.py:263
  73.4 14.9 %psum.22 = f32[2048]{0:T(1024)S(1)} all-reduce(f32[2048]{0:T(1024)S(1)} %fusion.4), channel_id=1, replica_groups={{1,2,5,6,9,10,13,14},{0,3,4,7,8,11,12,15},{17,18,21,22,25,26,29,30},{16..., use_global_device_ids=true, to_apply=%region_6.7 | all-reduce | flops 2048 | bytes 16384 | tf_op jit(solution)/shard_map/psum | solution.py:264
  88.3 1.5 all-to-all-done.2.refs_0_
  89.8 3.0 %shard_map.96 = (f32[32,32,128]{2,1,0:T(8,128)}, f32[16,128]{1,0:T(8,128)S(1)}, f32[32,128]{1,0:T(8,128)S(1)}) custom-call(s32[4,72]{1,0:T(4,128)S(1)} %add_add_fusion.work, bf16[32,72,128]{2,1,0:T(8,128)(2,1)S(1)} %all-to-all-done.catalog, bf16[2048,128]{1,0:T(8,128)(2,1)S(1)} %maximum_bitcast_fusion.viewers_t, f32[32,32,128]{2,1,0:T(8,128)S(1)} %all-to-all-done.2.refs_0_, ...), custom_call_target="tpu_custom_call" | custom-call | tf_op jit(solution)/shard_map/pallas_call | solution.py:221
  92.8 8.0 %all-to-all-start.3 = ((f32[32,32,128]{2,1,0:T(8,128)}), f32[32,32,128]{2,1,0:T(8,128)S(1)}, u32[]{:S(2)}, u32[]{:S(2)}) async-start(f32[32,32,128]{2,1,0:T(8,128)} %get-tuple-element.23), calls=%async_computation.3 | async-start | bytes 1048576 | tf_op jit(solution)/shard_map/all_to_all | solution.py:200
  100.8 1.8 %all-gather.2 = f32[32,128]{1,0:T(8,128)S(1)} all-gather(f32[16,128]{1,0:T(8,128)S(1)} %get-tuple-element.25), channel_id=4, replica_groups={{0,1},{2,3},{4,5},{6,7},{8,9},{10,11},{12,13},{14,15},{16,17},{18,19},{..., dimensions={0}, use_global_device_ids=true | all-gather | bytes 24576 | tf_op jit(solution)/shard_map/all_gather | solution.py:263
  102.6 13.8 %psum.23 = f32[2048]{0:T(1024)S(1)} all-reduce(f32[2048]{0:T(1024)S(1)} %fusion.3), channel_id=1, replica_groups={{1,2,5,6,9,10,13,14},{0,3,4,7,8,11,12,15},{17,18,21,22,25,26,29,30},{16..., use_global_device_ids=true, to_apply=%region_7.8 | all-reduce | flops 2048 | bytes 16384 | tf_op jit(solution)/shard_map/psum | solution.py:264
  116.5 2.5 %all-to-all-done.3.outlays = f32[32,32,128]{2,1,0:T(8,128)S(1)} async-done(((f32[32,32,128]{2,1,0:T(8,128)}), f32[32,32,128]{2,1,0:T(8,128)S(1)}, u32[]{:S(2)}, u32[]{:S(2)}) %all-to-all-start.3) | async-done | bytes 524320 | tf_op jit(solution)/shard_map/all_to_all | solution.py:200
  119.0 3.4 %shard_map.97 = (bf16[32,64,128]{2,1,0:T(8,128)(2,1)}, f32[1,128]{1,0:T(1,128)}, f32[16,128]{1,0:T(8,128)}, bf16[33,16,128]{2,1,0:T(8,128)(2,1)S(1)}) custom-call(s32[4,72]{1,0:T(4,128)S(1)} %add_add_fusion.work, s32[1]{0:T(128)} %bitcast.5.own, bf16[32,72,128]{2,1,0:T(8,128)(2,1)S(1)} %all-to-all-done.catalog, ...), custom_call_target="tpu_custom_call" | custom-call | tf_op jit(solution)/shard_map/pallas_call | solution.py:221
  122.4 2.9 %shard_map.98 = f32[2,8,64,128]{3,2,1,0:T(8,128)S(1)} custom-call(s32[4,72]{1,0:T(4,128)S(1)} %add_add_fusion.work, bf16[32,72,128]{2,1,0:T(8,128)(2,1)S(1)} %all-to-all-done.catalog, bf16[2048,128]{1,0:T(8,128)(2,1)S(1)} %maximum_bitcast_fusion.viewers_t, bf16[33,16,128]{2,1,0:T(8,128)(2,1)S(1)} %get-tuple-element.28.strips, f32[16,128]{1,0:T(8,128)S(1)} %fusion.7.duals), custom_call_target="tpu_custom_call" | custom-call | tf_op jit(solution)/shard_map/pallas_call | solution.py:221
  125.3 1.9 %collective-permute-start = (f32[8,64,128]{2,1,0:T(8,128)S(1)}, f32[8,64,128]{2,1,0:T(8,128)S(1)}, u32[]{:S(2)}, u32[]{:S(2)}) collective-permute-start(f32[8,64,128]{2,1,0:T(8,128)S(1)} %dynamic-slice_bitcast_fusion), channel_id=1, source_target_pairs={{0,1},{1,0},{2,3},{3,2},{4,5},{5,4},{6,7},{7,6},{8,9},{9,8},{10,11... | collective-permute-start | bytes 786440 | tf_op jit(solution)/shard_map/ppermute | solution.py:298
  127.3 1.5 collective-permute-done
  128.8 13.7 %all_to_all.30 = bf16[8,64,128]{2,1,0:T(8,128)(2,1)S(1)} all-to-all(bf16[8,64,128]{2,1,0:T(8,128)(2,1)S(1)} %fusion), channel_id=1, replica_groups={{1,2,5,6,9,10,13,14},{0,3,4,7,8,11,12,15},{17,18,21,22,25,26,29,30},{16..., dimensions={0} | all-to-all | bytes 262144 | tf_op jit(solution)/shard_map/all_to_all | solution.py:300
  142.6 7.1 %all-to-all-start.5 = ((bf16[32,64,128]{2,1,0:T(8,128)(2,1)}), bf16[32,64,128]{2,1,0:T(8,128)(2,1)S(1)}, u32[]{:S(2)}, u32[]{:S(2)}) async-start(bf16[32,64,128]{2,1,0:T(8,128)(2,1)} %get-tuple-element.29), calls=%async_computation.5 | async-start | bytes 1048576 | tf_op jit(solution)/shard_map/all_to_all | solution.py:200
  149.6 0.6 reduce_sum.74
  150.3 17.3 %all-to-all-done.5 = bf16[32,64,128]{2,1,0:T(8,128)(2,1)S(1)} async-done(((bf16[32,64,128]{2,1,0:T(8,128)(2,1)}), bf16[32,64,128]{2,1,0:T(8,128)(2,1)S(1)}, u32[]{:S(2)}, u32[]{:S(2)}) %all-to-all-start.5) | async-done | bytes 524320 | tf_op jit(solution)/shard_map/all_to_all | solution.py:200
  167.5 0.7 reduce_sum.75
  (19 shorter events, 0.2 us)
Async XLA Ops:
  2.2 15.3 %copy-start = (bf16[64,2048]{1,0:T(8,128)(2,1)S(1)}, bf16[64,2048]{1,0:T(8,128)(2,1)}, u32[]{:S(2)}) copy-start(bf16[64,2048]{1,0:T(8,128)(2,1)} %viewers.1) | copy-start | bytes 786436
  2.2 32.3 %all-to-all-start = ((bf16[32,72,128]{2,1,0:T(8,128)(2,1)}), bf16[32,72,128]{2,1,0:T(8,128)(2,1)S(1)}, u32[]{:S(2)}, u32[]{:S(2)}) async-start(bf16[32,72,128]{2,1,0:T(8,128)(2,1)} %shard_map.93), calls=%async_computation | async-start | bytes 1179648 | tf_op jit(solution)/shard_map/all_to_all | solution.py:200
  15.5 0.7 copy-start.2
  15.6 0.7 copy-start.3
  37.4 21.8 %all-to-all-start.1 = ((f32[32,32,128]{2,1,0:T(8,128)}), f32[32,32,128]{2,1,0:T(8,128)S(1)}, u32[]{:S(2)}, u32[]{:S(2)}) async-start(f32[32,32,128]{2,1,0:T(8,128)} %get-tuple-element.17), calls=%async_computation.1 | async-start | bytes 1048576 | tf_op jit(solution)/shard_map/all_to_all | solution.py:200
  44.0 15.1 %copy-start.1 = (f32[2048]{0:T(1024)S(1)}, f32[2048]{0:T(1024)}, u32[]{:S(2)}) copy-start(f32[2048]{0:T(1024)} %param.9) | copy-start | bytes 24580
  62.1 27.7 %all-to-all-start.2 = ((f32[32,32,128]{2,1,0:T(8,128)}), f32[32,32,128]{2,1,0:T(8,128)S(1)}, u32[]{:S(2)}, u32[]{:S(2)}) async-start(f32[32,32,128]{2,1,0:T(8,128)} %get-tuple-element.20), calls=%async_computation.2 | async-start | bytes 1048576 | tf_op jit(solution)/shard_map/all_to_all | solution.py:200
  92.8 26.2 %all-to-all-start.3 = ((f32[32,32,128]{2,1,0:T(8,128)}), f32[32,32,128]{2,1,0:T(8,128)S(1)}, u32[]{:S(2)}, u32[]{:S(2)}) async-start(f32[32,32,128]{2,1,0:T(8,128)} %get-tuple-element.23), calls=%async_computation.3 | async-start | bytes 1048576 | tf_op jit(solution)/shard_map/all_to_all | solution.py:200
  125.3 3.4 %collective-permute-start = (f32[8,64,128]{2,1,0:T(8,128)S(1)}, f32[8,64,128]{2,1,0:T(8,128)S(1)}, u32[]{:S(2)}, u32[]{:S(2)}) collective-permute-start(f32[8,64,128]{2,1,0:T(8,128)S(1)} %dynamic-slice_bitcast_fusion), channel_id=1, source_target_pairs={{0,1},{1,0},{2,3},{3,2},{4,5},{5,4},{6,7},{7,6},{8,9},{9,8},{10,11... | collective-permute-start | bytes 786440 | tf_op jit(solution)/shard_map/ppermute | solution.py:298
  142.6 25.0 %all-to-all-start.5 = ((bf16[32,64,128]{2,1,0:T(8,128)(2,1)}), bf16[32,64,128]{2,1,0:T(8,128)(2,1)S(1)}, u32[]{:S(2)}, u32[]{:S(2)}) async-start(bf16[32,64,128]{2,1,0:T(8,128)(2,1)} %get-tuple-element.29), calls=%async_computation.5 | async-start | bytes 1048576 | tf_op jit(solution)/shard_map/all_to_all | solution.py:200

commit v5 on v4

--- a/solution.py
+++ b/solution.py
@@ -180,7 +180,7 @@
 
     for_pairs(work, UNROLL, pairs)
     for group_no in range(imp_acc.shape[0]):
-        imp_out[ring_of(group_no), group_no // 2] = imp_acc[group_no]
+        imp_out[ring_of(group_no), group_no // 2 % 2, group_no // 4] = imp_acc[group_no]
 
 
 def chip_groups():
@@ -194,6 +194,16 @@
 def ring_groups():
     places = range(lax.axis_size(ADV))
     return [[place for place in places if ring_of(place) == ring] for ring in (0, 1)]
+
+
+def last_groups():
+    return [ring[parity::2] for ring in ring_groups() for parity in (0, 1)]
+
+
+def swapped(value, index, pairs):
+    kept = lax.dynamic_index_in_dim(value, index, 0, keepdims=False)
+    given = lax.dynamic_index_in_dim(value, 1 - index, 0, keepdims=False)
+    return kept + lax.ppermute(given, ADV, pairs)
 
 
 def to_all(value, axis):
@@ -288,16 +298,16 @@
     )
     adv_parts = to_all(adv_parts, IMP)
     (imp_parts,) = call(
-        imp_kernel, 1, [((2, groups // 2, features, GROUP), F32)],
+        imp_kernel, 1, [((2, 2, groups // 4, features, GROUP), F32)],
         [((groups, features, GROUP), F32)],
         work, catalog, viewers_t, strip_rows, duals,
     )
-    ring = ring_of(lax.axis_index(ADV))
-    kept = lax.dynamic_index_in_dim(imp_parts, ring, 0, keepdims=False)
-    given = lax.dynamic_index_in_dim(imp_parts, 1 - ring, 0, keepdims=False)
-    given = lax.ppermute(given, ADV, [(a, a ^ 1) for a in range(n_adv)])
-    imp_parts = (kept + given).astype(BF16)
-    imp_parts = lax.all_to_all(imp_parts, ADV, 0, 0, tiled=True, axis_index_groups=ring_groups())
+    place = lax.axis_index(ADV)
+    rings = ring_groups()
+    next_chip = [(ring[y], ring[y ^ 1]) for ring in rings for y in range(n_adv // 2)]
+    imp_parts = swapped(imp_parts, ring_of(place), [(a, a ^ 1) for a in range(n_adv)])
+    imp_parts = swapped(imp_parts, place // 2 % 2, next_chip).astype(BF16)
+    imp_parts = lax.all_to_all(imp_parts, ADV, 0, 0, tiled=True, axis_index_groups=last_groups())
     impression_grad = jnp.sum(imp_parts.astype(F32), axis=0).astype(BF16)
     advertiser_grad = jnp.sum(adv_parts.astype(F32), axis=0).astype(BF16)
     return own_prices.reshape(-1), out_duals.reshape(-1), impression_grad, advertiser_grad

time: 169 us -> 174 us (1.030)
  waiting for transfers between devices: 38.2 us -> 41.9 us
  starting transfers between devices: 44.5 us -> 47.2 us
    ppermute x1 -> x2, waiting for transfers between devices: 1.49 us -> 6.31 us  [swapped(): return kept + lax.ppermute(given, ADV, pairs)]
    ppermute x1 -> x2, starting transfers between devices: 1.92 us -> 4.43 us  [swapped(): return kept + lax.ppermute(given, ADV, pairs)]
  transfers between devices with their start and end apart: 6 -> 7, of which waited for: 6 -> 7; matrix products, arithmetic and copies ran while one was open for 2% -> 2% of each run, Pallas kernels for 0% -> 0%
where the time goes in v5:
time: 174 us; the launch traced here: 173 us
  blocking collectives  61.7 us (35%)
  starting transfers between devices  47.2 us (27%)
  waiting for transfers between devices  41.9 us (24%)
  Pallas kernels  16.6 us (10%)
  other arithmetic  2.71 us (2%)
  local copies, waits for them, and re-layouts  2.35 us (1%)
    psum x3, blocking collectives, meet(): lax.psum((pair[0] + pair[1]).reshape(-1), ADV, axis_index_groups=ring_gro...  43.8 us
    all_to_all x5, starting transfers between devices, to_all(): return lax.all_to_all(value, axis, 0, 0, tiled=True)  42.8 us
    all_to_all x5, waiting for transfers between devices, to_all(): return lax.all_to_all(value, axis, 0, 0, tiled=True)  35.6 us
    pallas_call x6, Pallas kernels, call(): pl.pallas_call(kernel, in_specs=[SMEM] * n_smem + [VMEM] * (len(args) - n...  16.6 us
    all_to_all x1, blocking collectives, local(): lax.all_to_all(imp_parts, ADV, 0, 0, tiled=True, axis_index_groups=last_g...  12.4 us
    ppermute x2, waiting for transfers between devices, swapped(): return kept + lax.ppermute(given, ADV, pairs)  6.31 us
    all_gather x3, blocking collectives, meet(): pair = lax.all_gather(demand, ADV, axis=0, axis_index_groups=chip_groups())  5.46 us
    ppermute x2, starting transfers between devices, swapped(): return kept + lax.ppermute(given, ADV, pairs)  4.43 us
  transfers between devices with their start and end apart: 7, of which 7 were waited for; matrix products, arithmetic and copies ran while one was open for 2% of the time, Pallas kernels for 0%

profile of v5, /device:TPU:8, one launch (start us, length us, event | category | flops | bytes accessed | tf_op | source)
XLA Modules:
  0.0 173.5 jit_solution(13743818290496762510)
XLA Ops:
  0.6 1.6 shard_map.93
  2.2 0.0 copy-start
  2.2 13.3 %all-to-all-start = ((bf16[32,72,128]{2,1,0:T(8,128)(2,1)}), bf16[32,72,128]{2,1,0:T(8,128)(2,1)S(1)}, u32[]{:S(2)}, u32[]{:S(2)}) async-start(bf16[32,72,128]{2,1,0:T(8,128)(2,1)} %shard_map.93), calls=%async_computation | async-start | bytes 1179648 | tf_op jit(solution)/shard_map/all_to_all | solution.py:210
  15.5 0.0 copy-start.2
  15.6 0.0 copy-start.3
  15.6 0.6 copy-done.2
  16.2 0.0 copy-done.3
  16.3 0.1 broadcast_compare_fusion
  16.4 0.7 convert_reduce_fusion.1
  17.1 0.1 lt.78
  17.2 0.1 copy.17
  17.3 0.1 sub.47
  17.4 0.1 copy.16
  17.4 0.1 sub.45
  17.5 0.0 copy-done
  17.5 0.3 copy.18
  17.8 0.1 pad.2.clone
  17.9 0.1 pad.1.clone
  18.0 0.7 pad.6.clone
  18.7 0.1 convert_reduce_fusion
  18.8 0.1 select_reduce_fusion.2
  19.0 0.1 add_add_fusion.work
  19.1 0.2 maximum_bitcast_fusion.viewers_t
  19.2 15.3 %all-to-all-done.catalog = bf16[32,72,128]{2,1,0:T(8,128)(2,1)S(1)} async-done(((bf16[32,72,128]{2,1,0:T(8,128)(2,1)}), bf16[32,72,128]{2,1,0:T(8,128)(2,1)S(1)}, u32[]{:S(2)}, u32[]{:S(2)}) %all-to-all-start) | async-done | bytes 589856 | tf_op jit(solution)/shard_map/all_to_all | solution.py:210
  34.5 2.8 %shard_map.94 = (f32[32,32,128]{2,1,0:T(8,128)}, f32[16,128]{1,0:T(8,128)S(1)}, f32[32,128]{1,0:T(8,128)S(1)}) custom-call(s32[4,72]{1,0:T(4,128)S(1)} %add_add_fusion.work, bf16[32,72,128]{2,1,0:T(8,128)(2,1)S(1)} %all-to-all-done.catalog, bf16[2048,128]{1,0:T(8,128)(2,1)S(1)} %maximum_bitcast_fusion.viewers_t), custom_call_target="tpu_custom_call" | custom-call | tf_op jit(solution)/shard_map/pallas_call | solution.py:231
  37.3 4.8 %all-to-all-start.1 = ((f32[32,32,128]{2,1,0:T(8,128)}), f32[32,32,128]{2,1,0:T(8,128)S(1)}, u32[]{:S(2)}, u32[]{:S(2)}) async-start(f32[32,32,128]{2,1,0:T(8,128)} %get-tuple-element.17), calls=%async_computation.1 | async-start | bytes 1048576 | tf_op jit(solution)/shard_map/all_to_all | solution.py:210
  42.2 1.8 %all-gather = f32[32,128]{1,0:T(8,128)S(1)} all-gather(f32[16,128]{1,0:T(8,128)S(1)} %get-tuple-element.19), channel_id=2, replica_groups={{0,1},{2,3},{4,5},{6,7},{8,9},{10,11},{12,13},{14,15},{16,17},{18,19},{..., dimensions={0}, use_global_device_ids=true | all-gather | bytes 24576 | tf_op jit(solution)/shard_map/all_gather | solution.py:273
  44.0 0.0 copy-start.1
  44.0 15.0 %psum.21 = f32[2048]{0:T(1024)S(1)} all-reduce(f32[2048]{0:T(1024)S(1)} %fusion.5), channel_id=1, replica_groups={{1,2,5,6,9,10,13,14},{0,3,4,7,8,11,12,15},{17,18,21,22,25,26,29,30},{16..., use_global_device_ids=true, to_apply=%region_5.6 | all-reduce | flops 2048 | bytes 16384 | tf_op jit(solution)/shard_map/psum | solution.py:274
  59.1 0.0 copy-done.1
  59.1 0.1 all-to-all-done.1.refs_0_
  59.2 3.0 %shard_map.95 = (f32[32,32,128]{2,1,0:T(8,128)}, f32[16,128]{1,0:T(8,128)S(1)}, f32[32,128]{1,0:T(8,128)S(1)}) custom-call(s32[4,72]{1,0:T(4,128)S(1)} %add_add_fusion.work, bf16[32,72,128]{2,1,0:T(8,128)(2,1)S(1)} %all-to-all-done.catalog, bf16[2048,128]{1,0:T(8,128)(2,1)S(1)} %maximum_bitcast_fusion.viewers_t, f32[32,32,128]{2,1,0:T(8,128)S(1)} %all-to-all-done.1.refs_0_, ...), custom_call_target="tpu_custom_call" | custom-call | tf_op jit(solution)/shard_map/pallas_call | solution.py:231
  62.1 9.4 %all-to-all-start.2 = ((f32[32,32,128]{2,1,0:T(8,128)}), f32[32,32,128]{2,1,0:T(8,128)S(1)}, u32[]{:S(2)}, u32[]{:S(2)}) async-start(f32[32,32,128]{2,1,0:T(8,128)} %get-tuple-element.20), calls=%async_computation.2 | async-start | bytes 1048576 | tf_op jit(solution)/shard_map/all_to_all | solution.py:210
  71.6 1.8 %all-gather.1 = f32[32,128]{1,0:T(8,128)S(1)} all-gather(f32[16,128]{1,0:T(8,128)S(1)} %get-tuple-element.22), channel_id=3, replica_groups={{0,1},{2,3},{4,5},{6,7},{8,9},{10,11},{12,13},{14,15},{16,17},{18,19},{..., dimensions={0}, use_global_device_ids=true | all-gather | bytes 24576 | tf_op jit(solution)/shard_map/all_gather | solution.py:273
  73.4 14.9 %psum.22 = f32[2048]{0:T(1024)S(1)} all-reduce(f32[2048]{0:T(1024)S(1)} %fusion.4), channel_id=1, replica_groups={{1,2,5,6,9,10,13,14},{0,3,4,7,8,11,12,15},{17,18,21,22,25,26,29,30},{16..., use_global_device_ids=true, to_apply=%region_6.7 | all-reduce | flops 2048 | bytes 16384 | tf_op jit(solution)/shard_map/psum | solution.py:274
  88.3 1.5 all-to-all-done.2.refs_0_
  89.8 3.0 %shard_map.96 = (f32[32,32,128]{2,1,0:T(8,128)}, f32[16,128]{1,0:T(8,128)S(1)}, f32[32,128]{1,0:T(8,128)S(1)}) custom-call(s32[4,72]{1,0:T(4,128)S(1)} %add_add_fusion.work, bf16[32,72,128]{2,1,0:T(8,128)(2,1)S(1)} %all-to-all-done.catalog, bf16[2048,128]{1,0:T(8,128)(2,1)S(1)} %maximum_bitcast_fusion.viewers_t, f32[32,32,128]{2,1,0:T(8,128)S(1)} %all-to-all-done.2.refs_0_, ...), custom_call_target="tpu_custom_call" | custom-call | tf_op jit(solution)/shard_map/pallas_call | solution.py:231
  92.8 8.0 %all-to-all-start.3 = ((f32[32,32,128]{2,1,0:T(8,128)}), f32[32,32,128]{2,1,0:T(8,128)S(1)}, u32[]{:S(2)}, u32[]{:S(2)}) async-start(f32[32,32,128]{2,1,0:T(8,128)} %get-tuple-element.23), calls=%async_computation.3 | async-start | bytes 1048576 | tf_op jit(solution)/shard_map/all_to_all | solution.py:210
  100.8 1.8 %all-gather.2 = f32[32,128]{1,0:T(8,128)S(1)} all-gather(f32[16,128]{1,0:T(8,128)S(1)} %get-tuple-element.25), channel_id=4, replica_groups={{0,1},{2,3},{4,5},{6,7},{8,9},{10,11},{12,13},{14,15},{16,17},{18,19},{..., dimensions={0}, use_global_device_ids=true | all-gather | bytes 24576 | tf_op jit(solution)/shard_map/all_gather | solution.py:273
  102.6 13.9 %psum.23 = f32[2048]{0:T(1024)S(1)} all-reduce(f32[2048]{0:T(1024)S(1)} %fusion.3), channel_id=1, replica_groups={{1,2,5,6,9,10,13,14},{0,3,4,7,8,11,12,15},{17,18,21,22,25,26,29,30},{16..., use_global_device_ids=true, to_apply=%region_7.8 | all-reduce | flops 2048 | bytes 16384 | tf_op jit(solution)/shard_map/psum | solution.py:274
  116.5 2.5 %all-to-all-done.3.outlays = f32[32,32,128]{2,1,0:T(8,128)S(1)} async-done(((f32[32,32,128]{2,1,0:T(8,128)}), f32[32,32,128]{2,1,0:T(8,128)S(1)}, u32[]{:S(2)}, u32[]{:S(2)}) %all-to-all-start.3) | async-done | bytes 524320 | tf_op jit(solution)/shard_map/all_to_all | solution.py:210
  119.0 3.4 %shard_map.97 = (bf16[32,64,128]{2,1,0:T(8,128)(2,1)}, f32[1,128]{1,0:T(1,128)}, f32[16,128]{1,0:T(8,128)}, bf16[33,16,128]{2,1,0:T(8,128)(2,1)S(1)}) custom-call(s32[4,72]{1,0:T(4,128)S(1)} %add_add_fusion.work, s32[1]{0:T(128)} %bitcast.5.own, bf16[32,72,128]{2,1,0:T(8,128)(2,1)S(1)} %all-to-all-done.catalog, ...), custom_call_target="tpu_custom_call" | custom-call | tf_op jit(solution)/shard_map/pallas_call | solution.py:231
  122.4 2.9 %shard_map.98 = f32[2,2,4,64,128]{4,3,2,1,0:T(8,128)S(1)} custom-call(s32[4,72]{1,0:T(4,128)S(1)} %add_add_fusion.work, bf16[32,72,128]{2,1,0:T(8,128)(2,1)S(1)} %all-to-all-done.catalog, bf16[2048,128]{1,0:T(8,128)(2,1)S(1)} %maximum_bitcast_fusion.viewers_t, bf16[33,16,128]{2,1,0:T(8,128)(2,1)S(1)} %get-tuple-element.28.strips, f32[16,128]{1,0:T(8,128)S(1)} %fusion.7.duals), custom_call_target="tpu_custom_call" | custom-call | tf_op jit(solution)/shard_map/pallas_call | solution.py:231
  125.3 1.9 %collective-permute-start = (f32[2,4,64,128]{3,2,1,0:T(8,128)S(1)}, f32[2,4,64,128]{3,2,1,0:T(8,128)S(1)}, u32[]{:S(2)}, u32[]{:S(2)}) collective-permute-start(f32[2,4,64,128]{3,2,1,0:T(8,128)S(1)} %dynamic-slice_bitcast_fusion), channel_id=1, source_target_pairs={{0,1},{1,0},{2,3},{3,2},{4,5},{5,4},{6,7},{7,6},{8,9},{9,8},{10,11... | collective-permute-start | bytes 786440 | tf_op jit(solution)/shard_map/ppermute | solution.py:206
  127.3 1.5 collective-permute-done
  128.8 2.5 %collective-permute-start.1 = (f32[4,64,128]{2,1,0:T(8,128)S(1)}, f32[4,64,128]{2,1,0:T(8,128)S(1)}, u32[]{:S(2)}, u32[]{:S(2)}) collective-permute-start(f32[4,64,128]{2,1,0:T(8,128)S(1)} %dynamic-slice_bitcast_fusion.1), channel_id=1, source_target_pairs={{1,2},{2,1},{5,6},{6,5},{9,10},{10,9},{13,14},{14,13},{0,3},{3,0},... | collective-permute-start | bytes 393224 | tf_op jit(solution)/shard_map/ppermute | solution.py:206
  131.4 4.8 %collective-permute-done.1 = f32[4,64,128]{2,1,0:T(8,128)S(1)} collective-permute-done((f32[4,64,128]{2,1,0:T(8,128)S(1)}, f32[4,64,128]{2,1,0:T(8,128)S(1)}, u32[]{:S(2)}, u32[]{:S(2)}) %collective-permute-start.1) | collective-permute-done | bytes 131104 | tf_op jit(solution)/shard_map/ppermute | solution.py:206
  136.2 12.4 %all_to_all.30 = bf16[4,64,128]{2,1,0:T(8,128)(2,1)S(1)} all-to-all(bf16[4,64,128]{2,1,0:T(8,128)(2,1)S(1)} %fusion), channel_id=1, replica_groups={{1,5,9,13},{2,6,10,14},{0,4,8,12},{3,7,11,15},{17,21,25,29},{18,22,26,3..., dimensions={0} | all-to-all | bytes 131072 | tf_op jit(solution)/shard_map/all_to_all | solution.py:310
  148.7 7.3 %all-to-all-start.5 = ((bf16[32,64,128]{2,1,0:T(8,128)(2,1)}), bf16[32,64,128]{2,1,0:T(8,128)(2,1)S(1)}, u32[]{:S(2)}, u32[]{:S(2)}) async-start(bf16[32,64,128]{2,1,0:T(8,128)(2,1)} %get-tuple-element.29), calls=%async_computation.5 | async-start | bytes 1048576 | tf_op jit(solution)/shard_map/all_to_all | solution.py:210
  155.9 0.6 reduce_sum.74
  156.5 16.2 %all-to-all-done.5 = bf16[32,64,128]{2,1,0:T(8,128)(2,1)S(1)} async-done(((bf16[32,64,128]{2,1,0:T(8,128)(2,1)}), bf16[32,64,128]{2,1,0:T(8,128)(2,1)S(1)}, u32[]{:S(2)}, u32[]{:S(2)}) %all-to-all-start.5) | async-done | bytes 524320 | tf_op jit(solution)/shard_map/all_to_all | solution.py:210
  172.8 0.7 reduce_sum.75
  (21 shorter events, 0.2 us)
Async XLA Ops:
  2.2 15.3 %copy-start = (bf16[64,2048]{1,0:T(8,128)(2,1)S(1)}, bf16[64,2048]{1,0:T(8,128)(2,1)}, u32[]{:S(2)}) copy-start(bf16[64,2048]{1,0:T(8,128)(2,1)} %viewers.1) | copy-start | bytes 786436
  2.2 32.3 %all-to-all-start = ((bf16[32,72,128]{2,1,0:T(8,128)(2,1)}), bf16[32,72,128]{2,1,0:T(8,128)(2,1)S(1)}, u32[]{:S(2)}, u32[]{:S(2)}) async-start(bf16[32,72,128]{2,1,0:T(8,128)(2,1)} %shard_map.93), calls=%async_computation | async-start | bytes 1179648 | tf_op jit(solution)/shard_map/all_to_all | solution.py:210
  15.5 0.7 copy-start.2
  15.6 0.7 copy-start.3
  37.3 21.8 %all-to-all-start.1 = ((f32[32,32,128]{2,1,0:T(8,128)}), f32[32,32,128]{2,1,0:T(8,128)S(1)}, u32[]{:S(2)}, u32[]{:S(2)}) async-start(f32[32,32,128]{2,1,0:T(8,128)} %get-tuple-element.17), calls=%async_computation.1 | async-start | bytes 1048576 | tf_op jit(solution)/shard_map/all_to_all | solution.py:210
  44.0 15.1 %copy-start.1 = (f32[2048]{0:T(1024)S(1)}, f32[2048]{0:T(1024)}, u32[]{:S(2)}) copy-start(f32[2048]{0:T(1024)} %param.9) | copy-start | bytes 24580
  62.1 27.7 %all-to-all-start.2 = ((f32[32,32,128]{2,1,0:T(8,128)}), f32[32,32,128]{2,1,0:T(8,128)S(1)}, u32[]{:S(2)}, u32[]{:S(2)}) async-start(f32[32,32,128]{2,1,0:T(8,128)} %get-tuple-element.20), calls=%async_computation.2 | async-start | bytes 1048576 | tf_op jit(solution)/shard_map/all_to_all | solution.py:210
  92.8 26.2 %all-to-all-start.3 = ((f32[32,32,128]{2,1,0:T(8,128)}), f32[32,32,128]{2,1,0:T(8,128)S(1)}, u32[]{:S(2)}, u32[]{:S(2)}) async-start(f32[32,32,128]{2,1,0:T(8,128)} %get-tuple-element.23), calls=%async_computation.3 | async-start | bytes 1048576 | tf_op jit(solution)/shard_map/all_to_all | solution.py:210
  125.3 3.4 %collective-permute-start = (f32[2,4,64,128]{3,2,1,0:T(8,128)S(1)}, f32[2,4,64,128]{3,2,1,0:T(8,128)S(1)}, u32[]{:S(2)}, u32[]{:S(2)}) collective-permute-start(f32[2,4,64,128]{3,2,1,0:T(8,128)S(1)} %dynamic-slice_bitcast_fusion), channel_id=1, source_target_pairs={{0,1},{1,0},{2,3},{3,2},{4,5},{5,4},{6,7},{7,6},{8,9},{9,8},{10,11... | collective-permute-start | bytes 786440 | tf_op jit(solution)/shard_map/ppermute | solution.py:206
  128.8 7.4 %collective-permute-start.1 = (f32[4,64,128]{2,1,0:T(8,128)S(1)}, f32[4,64,128]{2,1,0:T(8,128)S(1)}, u32[]{:S(2)}, u32[]{:S(2)}) collective-permute-start(f32[4,64,128]{2,1,0:T(8,128)S(1)} %dynamic-slice_bitcast_fusion.1), channel_id=1, source_target_pairs={{1,2},{2,1},{5,6},{6,5},{9,10},{10,9},{13,14},{14,13},{0,3},{3,0},... | collective-permute-start | bytes 393224 | tf_op jit(solution)/shard_map/ppermute | solution.py:206
  148.7 24.1 %all-to-all-start.5 = ((bf16[32,64,128]{2,1,0:T(8,128)(2,1)}), bf16[32,64,128]{2,1,0:T(8,128)(2,1)S(1)}, u32[]{:S(2)}, u32[]{:S(2)}) async-start(bf16[32,64,128]{2,1,0:T(8,128)(2,1)} %get-tuple-element.29), calls=%async_computation.5 | async-start | bytes 1048576 | tf_op jit(solution)/shard_map/all_to_all | solution.py:210

commit v6 on v5

--- a/solution.py
+++ b/solution.py
@@ -12,12 +12,13 @@
 BLOCK = 128
 PARTS = 8
 STRIP = 16
-UNROLL = 24
+UNROLL = 22
 DEAD = 1e30
 
 F32 = jnp.float32
 BF16 = jnp.bfloat16
-IMP = ("z", "x")
+IMP = "imp"
+ROW = 4
 ADV = "adv"
 VMEM = pl.BlockSpec(memory_space=pltpu.VMEM)
 SMEM = pl.BlockSpec(memory_space=pltpu.SMEM)
@@ -206,8 +207,14 @@
     return kept + lax.ppermute(given, ADV, pairs)
 
 
-def to_all(value, axis):
-    return lax.all_to_all(value, axis, 0, 0, tiled=True)
+def snake(index):
+    row, place = index // ROW, index % ROW
+    return row * ROW + place + row % 2 * (ROW - 1 - 2 * place)
+
+
+def to_peers(value):
+    order = [snake(index) for index in range(lax.axis_size(IMP))]
+    return lax.all_to_all(value, IMP, 0, 0, tiled=True, axis_index_groups=[order])
 
 
 def work_list(ids, counts, dead):
@@ -242,8 +249,8 @@
     features = impression_vectors.shape[0]
     groups, _, slots = blocks.shape
     n_imp, n_adv = lax.axis_size(IMP), lax.axis_size(ADV)
-    work = work_list(blocks.reshape(groups, slots) // n_adv, counts, n_imp)
-    own = lax.axis_index(IMP).astype(jnp.int32).reshape(1)
+    work = work_list(snake(blocks.reshape(groups, slots) // n_adv), counts, n_imp)
+    own = snake(lax.axis_index(IMP)).astype(jnp.int32).reshape(1)
     caps = capacity.reshape(groups, GROUP)
     ones = jnp.ones((3, impression_vectors.shape[1]), BF16)
     rest = STRIP - 3 + 3 * groups
@@ -254,7 +261,7 @@
         pack_kernel, 0, [((n_imp, features + PARTS, BLOCK), BF16)], [],
         advertiser_vectors, spend_limits.reshape(1, BLOCK), params=None,
     )
-    catalog = to_all(packed, IMP)
+    catalog = to_peers(packed)
 
     exchange = [((n_imp, n_imp, BLOCK), F32), ((groups, GROUP), F32)]
     levels = [((n_imp, BLOCK), F32)]
@@ -269,7 +276,7 @@
     duals = jnp.zeros((groups, GROUP), F32)
 
     def meet(outlays, demand, duals):
-        outlays = to_all(outlays, IMP)
+        outlays = to_peers(outlays)
         pair = lax.all_gather(demand, ADV, axis=0, axis_index_groups=chip_groups())
         demand = lax.psum(
             (pair[0] + pair[1]).reshape(-1), ADV, axis_index_groups=ring_groups()
@@ -296,7 +303,7 @@
         [((n_imp + 1, features, BLOCK), F32)] + levels,
         work, own, catalog, viewers_t, impression_vectors, outlays, prices, rate, duals,
     )
-    adv_parts = to_all(adv_parts, IMP)
+    adv_parts = to_peers(adv_parts)
     (imp_parts,) = call(
         imp_kernel, 1, [((2, 2, groups // 4, features, GROUP), F32)],
         [((groups, features, GROUP), F32)],
@@ -314,19 +321,17 @@
 
 
 def solution(mesh):
-    n_imp, n_adv = (mesh.shape[axis] for axis in ("imp", "adv"))
-    chips = jax.sharding.Mesh(mesh.devices.reshape(n_imp // 4, 4, n_adv), IMP + (ADV,))
     return jax.shard_map(
         local,
-        mesh=chips,
+        mesh=mesh,
         in_specs=(
             P(None, IMP),
-            P(None, IMP + (ADV,)),
-            P(IMP + (ADV,)),
+            P(None, (IMP, ADV)),
+            P((IMP, ADV)),
             P(IMP),
             P(IMP, ADV, None),
             P(IMP, ADV),
         ),
-        out_specs=(P(IMP + (ADV,)), P(IMP), P(None, IMP + (ADV,)), P(None, IMP + (ADV,))),
+        out_specs=(P((IMP, ADV)), P(IMP), P(None, (IMP, ADV)), P(None, (IMP, ADV))),
         check_vma=False,
     )

time: 174 us -> 174 us (level)
  no operation moved by 1% of the time
where the time goes in v6:
time: 174 us; the launch traced here: 173 us
  blocking collectives  61.7 us (35%)
  starting transfers between devices  46.7 us (27%)
  waiting for transfers between devices  42.3 us (24%)
  Pallas kernels  16.1 us (9%)
  other arithmetic  2.72 us (2%)
  local copies, waits for them, and re-layouts  2.34 us (1%)
    psum x3, blocking collectives, meet(): lax.psum((pair[0] + pair[1]).reshape(-1), ADV, axis_index_groups=ring_gro...  43.7 us
    all_to_all x5, starting transfers between devices, to_peers(): lax.all_to_all(value, IMP, 0, 0, tiled=True, axis_index_groups=[order])  42.3 us
    all_to_all x5, waiting for transfers between devices, to_peers(): lax.all_to_all(value, IMP, 0, 0, tiled=True, axis_index_groups=[order])  36 us
    pallas_call x6, Pallas kernels, call(): pl.pallas_call(kernel, in_specs=[SMEM] * n_smem + [VMEM] * (len(args) - n...  16.1 us
    all_to_all x1, blocking collectives, local(): lax.all_to_all(imp_parts, ADV, 0, 0, tiled=True, axis_index_groups=last_g...  12.4 us
    ppermute x2, waiting for transfers between devices, swapped(): return kept + lax.ppermute(given, ADV, pairs)  6.34 us
    all_gather x3, blocking collectives, meet(): pair = lax.all_gather(demand, ADV, axis=0, axis_index_groups=chip_groups())  5.46 us
    ppermute x2, starting transfers between devices, swapped(): return kept + lax.ppermute(given, ADV, pairs)  4.41 us
  transfers between devices with their start and end apart: 7, of which 7 were waited for; matrix products, arithmetic and copies ran while one was open for 2% of the time, Pallas kernels for 0%

profile of v6, /device:TPU:8, one launch (start us, length us, event | category | flops | bytes accessed | tf_op | source)
XLA Modules:
  0.0 172.8 jit_solution(7482381865031924776)
XLA Ops:
  0.6 1.6 shard_map.93
  2.2 0.0 copy-start
  2.2 13.3 %all-to-all-start = ((bf16[32,72,128]{2,1,0:T(8,128)(2,1)}), bf16[32,72,128]{2,1,0:T(8,128)(2,1)S(1)}, u32[]{:S(2)}, u32[]{:S(2)}) async-start(bf16[32,72,128]{2,1,0:T(8,128)(2,1)} %shard_map.93), calls=%async_computation | async-start | bytes 1179648 | tf_op jit(solution)/shard_map/all_to_all | solution.py:217
  15.5 0.0 copy-start.2
  15.6 0.0 copy-start.3
  15.6 0.6 copy-done.2
  16.2 0.0 copy-done.3
  16.3 0.1 broadcast_compare_fusion
  16.4 0.7 convert_reduce_fusion.1
  17.1 0.1 lt.96
  17.2 0.1 copy.17
  17.3 0.1 sub.63
  17.4 0.1 copy.16
  17.5 0.1 sub.61
  17.5 0.0 copy-done
  17.6 0.3 copy.18
  17.8 0.1 pad.2.clone
  17.9 0.1 pad.1.clone
  18.0 0.7 pad.6.clone
  18.7 0.1 convert_reduce_fusion
  18.8 0.1 select_reduce_fusion.2
  19.0 0.1 add_add_fusion.work
  19.1 0.2 maximum_bitcast_fusion.viewers_t
  19.2 15.4 %all-to-all-done.catalog = bf16[32,72,128]{2,1,0:T(8,128)(2,1)S(1)} async-done(((bf16[32,72,128]{2,1,0:T(8,128)(2,1)}), bf16[32,72,128]{2,1,0:T(8,128)(2,1)S(1)}, u32[]{:S(2)}, u32[]{:S(2)}) %all-to-all-start) | async-done | bytes 589856 | tf_op jit(solution)/shard_map/all_to_all | solution.py:217
  34.7 2.7 %shard_map.94 = (f32[32,32,128]{2,1,0:T(8,128)}, f32[16,128]{1,0:T(8,128)S(1)}, f32[32,128]{1,0:T(8,128)S(1)}) custom-call(s32[4,66]{1,0:T(4,128)S(1)} %add_add_fusion.work, bf16[32,72,128]{2,1,0:T(8,128)(2,1)S(1)} %all-to-all-done.catalog, bf16[2048,128]{1,0:T(8,128)(2,1)S(1)} %maximum_bitcast_fusion.viewers_t), custom_call_target="tpu_custom_call" | custom-call | tf_op jit(solution)/shard_map/pallas_call | solution.py:238
  37.4 4.3 %all-to-all-start.1 = ((f32[32,32,128]{2,1,0:T(8,128)}), f32[32,32,128]{2,1,0:T(8,128)S(1)}, u32[]{:S(2)}, u32[]{:S(2)}) async-start(f32[32,32,128]{2,1,0:T(8,128)} %get-tuple-element.17), calls=%async_computation.1 | async-start | bytes 1048576 | tf_op jit(solution)/shard_map/all_to_all | solution.py:217
  41.8 1.8 %all-gather = f32[32,128]{1,0:T(8,128)S(1)} all-gather(f32[16,128]{1,0:T(8,128)S(1)} %get-tuple-element.19), channel_id=2, replica_groups={{0,1},{2,3},{4,5},{6,7},{8,9},{10,11},{12,13},{14,15},{16,17},{18,19},{..., dimensions={0}, use_global_device_ids=true | all-gather | bytes 24576 | tf_op jit(solution)/shard_map/all_gather | solution.py:280
  43.6 0.0 copy-start.1
  43.6 15.0 %psum.21 = f32[2048]{0:T(1024)S(1)} all-reduce(f32[2048]{0:T(1024)S(1)} %fusion.5), channel_id=1, replica_groups={{1,2,5,6,9,10,13,14},{0,3,4,7,8,11,12,15},{17,18,21,22,25,26,29,30},{16..., use_global_device_ids=true, to_apply=%region_5.6 | all-reduce | flops 2048 | bytes 16384 | tf_op jit(solution)/shard_map/psum | solution.py:281
  58.6 0.0 copy-done.1
  58.6 0.3 all-to-all-done.1.refs_0_
  58.9 2.9 %shard_map.95 = (f32[32,32,128]{2,1,0:T(8,128)}, f32[16,128]{1,0:T(8,128)S(1)}, f32[32,128]{1,0:T(8,128)S(1)}) custom-call(s32[4,66]{1,0:T(4,128)S(1)} %add_add_fusion.work, bf16[32,72,128]{2,1,0:T(8,128)(2,1)S(1)} %all-to-all-done.catalog, bf16[2048,128]{1,0:T(8,128)(2,1)S(1)} %maximum_bitcast_fusion.viewers_t, f32[32,32,128]{2,1,0:T(8,128)S(1)} %all-to-all-done.1.refs_0_, ...), custom_call_target="tpu_custom_call" | custom-call | tf_op jit(solution)/shard_map/pallas_call | solution.py:238
  61.8 9.2 %all-to-all-start.2 = ((f32[32,32,128]{2,1,0:T(8,128)}), f32[32,32,128]{2,1,0:T(8,128)S(1)}, u32[]{:S(2)}, u32[]{:S(2)}) async-start(f32[32,32,128]{2,1,0:T(8,128)} %get-tuple-element.20), calls=%async_computation.2 | async-start | bytes 1048576 | tf_op jit(solution)/shard_map/all_to_all | solution.py:217
  71.0 1.8 %all-gather.1 = f32[32,128]{1,0:T(8,128)S(1)} all-gather(f32[16,128]{1,0:T(8,128)S(1)} %get-tuple-element.22), channel_id=3, replica_groups={{0,1},{2,3},{4,5},{6,7},{8,9},{10,11},{12,13},{14,15},{16,17},{18,19},{..., dimensions={0}, use_global_device_ids=true | all-gather | bytes 24576 | tf_op jit(solution)/shard_map/all_gather | solution.py:280
  72.8 14.9 %psum.22 = f32[2048]{0:T(1024)S(1)} all-reduce(f32[2048]{0:T(1024)S(1)} %fusion.4), channel_id=1, replica_groups={{1,2,5,6,9,10,13,14},{0,3,4,7,8,11,12,15},{17,18,21,22,25,26,29,30},{16..., use_global_device_ids=true, to_apply=%region_6.7 | all-reduce | flops 2048 | bytes 16384 | tf_op jit(solution)/shard_map/psum | solution.py:281
  87.8 1.4 all-to-all-done.2.refs_0_
  89.2 2.9 %shard_map.96 = (f32[32,32,128]{2,1,0:T(8,128)}, f32[16,128]{1,0:T(8,128)S(1)}, f32[32,128]{1,0:T(8,128)S(1)}) custom-call(s32[4,66]{1,0:T(4,128)S(1)} %add_add_fusion.work, bf16[32,72,128]{2,1,0:T(8,128)(2,1)S(1)} %all-to-all-done.catalog, bf16[2048,128]{1,0:T(8,128)(2,1)S(1)} %maximum_bitcast_fusion.viewers_t, f32[32,32,128]{2,1,0:T(8,128)S(1)} %all-to-all-done.2.refs_0_, ...), custom_call_target="tpu_custom_call" | custom-call | tf_op jit(solution)/shard_map/pallas_call | solution.py:238
  92.1 8.1 %all-to-all-start.3 = ((f32[32,32,128]{2,1,0:T(8,128)}), f32[32,32,128]{2,1,0:T(8,128)S(1)}, u32[]{:S(2)}, u32[]{:S(2)}) async-start(f32[32,32,128]{2,1,0:T(8,128)} %get-tuple-element.23), calls=%async_computation.3 | async-start | bytes 1048576 | tf_op jit(solution)/shard_map/all_to_all | solution.py:217
  100.2 1.8 %all-gather.2 = f32[32,128]{1,0:T(8,128)S(1)} all-gather(f32[16,128]{1,0:T(8,128)S(1)} %get-tuple-element.25), channel_id=4, replica_groups={{0,1},{2,3},{4,5},{6,7},{8,9},{10,11},{12,13},{14,15},{16,17},{18,19},{..., dimensions={0}, use_global_device_ids=true | all-gather | bytes 24576 | tf_op jit(solution)/shard_map/all_gather | solution.py:280
  102.0 13.8 %psum.23 = f32[2048]{0:T(1024)S(1)} all-reduce(f32[2048]{0:T(1024)S(1)} %fusion.3), channel_id=1, replica_groups={{1,2,5,6,9,10,13,14},{0,3,4,7,8,11,12,15},{17,18,21,22,25,26,29,30},{16..., use_global_device_ids=true, to_apply=%region_7.8 | all-reduce | flops 2048 | bytes 16384 | tf_op jit(solution)/shard_map/psum | solution.py:281
  115.9 2.4 %all-to-all-done.3.outlays = f32[32,32,128]{2,1,0:T(8,128)S(1)} async-done(((f32[32,32,128]{2,1,0:T(8,128)}), f32[32,32,128]{2,1,0:T(8,128)S(1)}, u32[]{:S(2)}, u32[]{:S(2)}) %all-to-all-start.3) | async-done | bytes 524320 | tf_op jit(solution)/shard_map/all_to_all | solution.py:217
  118.3 3.3 %shard_map.97 = (bf16[32,64,128]{2,1,0:T(8,128)(2,1)}, f32[1,128]{1,0:T(1,128)}, f32[16,128]{1,0:T(8,128)}, bf16[33,16,128]{2,1,0:T(8,128)(2,1)S(1)}) custom-call(s32[4,66]{1,0:T(4,128)S(1)} %add_add_fusion.work, s32[1]{0:T(128)} %bitcast.5.own, bf16[32,72,128]{2,1,0:T(8,128)(2,1)S(1)} %all-to-all-done.catalog, ...), custom_call_target="tpu_custom_call" | custom-call | tf_op jit(solution)/shard_map/pallas_call | solution.py:238
  121.5 2.8 %shard_map.98 = f32[2,2,4,64,128]{4,3,2,1,0:T(8,128)S(1)} custom-call(s32[4,66]{1,0:T(4,128)S(1)} %add_add_fusion.work, bf16[32,72,128]{2,1,0:T(8,128)(2,1)S(1)} %all-to-all-done.catalog, bf16[2048,128]{1,0:T(8,128)(2,1)S(1)} %maximum_bitcast_fusion.viewers_t, bf16[33,16,128]{2,1,0:T(8,128)(2,1)S(1)} %get-tuple-element.28.strips, f32[16,128]{1,0:T(8,128)S(1)} %fusion.7.duals), custom_call_target="tpu_custom_call" | custom-call | tf_op jit(solution)/shard_map/pallas_call | solution.py:238
  124.3 1.9 %collective-permute-start = (f32[2,4,64,128]{3,2,1,0:T(8,128)S(1)}, f32[2,4,64,128]{3,2,1,0:T(8,128)S(1)}, u32[]{:S(2)}, u32[]{:S(2)}) collective-permute-start(f32[2,4,64,128]{3,2,1,0:T(8,128)S(1)} %dynamic-slice_bitcast_fusion), channel_id=1, source_target_pairs={{0,1},{1,0},{2,3},{3,2},{4,5},{5,4},{6,7},{7,6},{8,9},{9,8},{10,11... | collective-permute-start | bytes 786440 | tf_op jit(solution)/shard_map/ppermute | solution.py:207
  126.3 1.5 collective-permute-done
  127.8 2.5 %collective-permute-start.1 = (f32[4,64,128]{2,1,0:T(8,128)S(1)}, f32[4,64,128]{2,1,0:T(8,128)S(1)}, u32[]{:S(2)}, u32[]{:S(2)}) collective-permute-start(f32[4,64,128]{2,1,0:T(8,128)S(1)} %dynamic-slice_bitcast_fusion.1), channel_id=1, source_target_pairs={{1,2},{2,1},{5,6},{6,5},{9,10},{10,9},{13,14},{14,13},{0,3},{3,0},... | collective-permute-start | bytes 393224 | tf_op jit(solution)/shard_map/ppermute | solution.py:207
  130.3 4.9 %collective-permute-done.1 = f32[4,64,128]{2,1,0:T(8,128)S(1)} collective-permute-done((f32[4,64,128]{2,1,0:T(8,128)S(1)}, f32[4,64,128]{2,1,0:T(8,128)S(1)}, u32[]{:S(2)}, u32[]{:S(2)}) %collective-permute-start.1) | collective-permute-done | bytes 131104 | tf_op jit(solution)/shard_map/ppermute | solution.py:207
  135.2 12.4 %all_to_all.30 = bf16[4,64,128]{2,1,0:T(8,128)(2,1)S(1)} all-to-all(bf16[4,64,128]{2,1,0:T(8,128)(2,1)S(1)} %fusion), channel_id=1, replica_groups={{1,5,9,13},{2,6,10,14},{0,4,8,12},{3,7,11,15},{17,21,25,29},{18,22,26,3..., dimensions={0} | all-to-all | bytes 131072 | tf_op jit(solution)/shard_map/all_to_all | solution.py:317
  147.7 7.4 %all-to-all-start.5 = ((bf16[32,64,128]{2,1,0:T(8,128)(2,1)}), bf16[32,64,128]{2,1,0:T(8,128)(2,1)S(1)}, u32[]{:S(2)}, u32[]{:S(2)}) async-start(bf16[32,64,128]{2,1,0:T(8,128)(2,1)} %get-tuple-element.29), calls=%async_computation.5 | async-start | bytes 1048576 | tf_op jit(solution)/shard_map/all_to_all | solution.py:217
  155.0 0.6 reduce_sum.74
  155.7 16.4 %all-to-all-done.5 = bf16[32,64,128]{2,1,0:T(8,128)(2,1)S(1)} async-done(((bf16[32,64,128]{2,1,0:T(8,128)(2,1)}), bf16[32,64,128]{2,1,0:T(8,128)(2,1)S(1)}, u32[]{:S(2)}, u32[]{:S(2)}) %all-to-all-start.5) | async-done | bytes 524320 | tf_op jit(solution)/shard_map/all_to_all | solution.py:217
  172.1 0.7 reduce_sum.75
  (21 shorter events, 0.2 us)
Async XLA Ops:
  2.2 15.3 %copy-start = (bf16[64,2048]{1,0:T(8,128)(2,1)S(1)}, bf16[64,2048]{1,0:T(8,128)(2,1)}, u32[]{:S(2)}) copy-start(bf16[64,2048]{1,0:T(8,128)(2,1)} %viewers.1) | copy-start | bytes 786436
  2.2 32.4 %all-to-all-start = ((bf16[32,72,128]{2,1,0:T(8,128)(2,1)}), bf16[32,72,128]{2,1,0:T(8,128)(2,1)S(1)}, u32[]{:S(2)}, u32[]{:S(2)}) async-start(bf16[32,72,128]{2,1,0:T(8,128)(2,1)} %shard_map.93), calls=%async_computation | async-start | bytes 1179648 | tf_op jit(solution)/shard_map/all_to_all | solution.py:217
  15.5 0.7 copy-start.2
  15.6 0.7 copy-start.3
  37.4 21.5 %all-to-all-start.1 = ((f32[32,32,128]{2,1,0:T(8,128)}), f32[32,32,128]{2,1,0:T(8,128)S(1)}, u32[]{:S(2)}, u32[]{:S(2)}) async-start(f32[32,32,128]{2,1,0:T(8,128)} %get-tuple-element.17), calls=%async_computation.1 | async-start | bytes 1048576 | tf_op jit(solution)/shard_map/all_to_all | solution.py:217
  43.6 15.0 %copy-start.1 = (f32[2048]{0:T(1024)S(1)}, f32[2048]{0:T(1024)}, u32[]{:S(2)}) copy-start(f32[2048]{0:T(1024)} %param.9) | copy-start | bytes 24580
  61.8 27.4 %all-to-all-start.2 = ((f32[32,32,128]{2,1,0:T(8,128)}), f32[32,32,128]{2,1,0:T(8,128)S(1)}, u32[]{:S(2)}, u32[]{:S(2)}) async-start(f32[32,32,128]{2,1,0:T(8,128)} %get-tuple-element.20), calls=%async_computation.2 | async-start | bytes 1048576 | tf_op jit(solution)/shard_map/all_to_all | solution.py:217
  92.1 26.2 %all-to-all-start.3 = ((f32[32,32,128]{2,1,0:T(8,128)}), f32[32,32,128]{2,1,0:T(8,128)S(1)}, u32[]{:S(2)}, u32[]{:S(2)}) async-start(f32[32,32,128]{2,1,0:T(8,128)} %get-tuple-element.23), calls=%async_computation.3 | async-start | bytes 1048576 | tf_op jit(solution)/shard_map/all_to_all | solution.py:217
  124.3 3.4 %collective-permute-start = (f32[2,4,64,128]{3,2,1,0:T(8,128)S(1)}, f32[2,4,64,128]{3,2,1,0:T(8,128)S(1)}, u32[]{:S(2)}, u32[]{:S(2)}) collective-permute-start(f32[2,4,64,128]{3,2,1,0:T(8,128)S(1)} %dynamic-slice_bitcast_fusion), channel_id=1, source_target_pairs={{0,1},{1,0},{2,3},{3,2},{4,5},{5,4},{6,7},{7,6},{8,9},{9,8},{10,11... | collective-permute-start | bytes 786440 | tf_op jit(solution)/shard_map/ppermute | solution.py:207
  127.8 7.4 %collective-permute-start.1 = (f32[4,64,128]{2,1,0:T(8,128)S(1)}, f32[4,64,128]{2,1,0:T(8,128)S(1)}, u32[]{:S(2)}, u32[]{:S(2)}) collective-permute-start(f32[4,64,128]{2,1,0:T(8,128)S(1)} %dynamic-slice_bitcast_fusion.1), channel_id=1, source_target_pairs={{1,2},{2,1},{5,6},{6,5},{9,10},{10,9},{13,14},{14,13},{0,3},{3,0},... | collective-permute-start | bytes 393224 | tf_op jit(solution)/shard_map/ppermute | solution.py:207
  147.7 24.4 %all-to-all-start.5 = ((bf16[32,64,128]{2,1,0:T(8,128)(2,1)}), bf16[32,64,128]{2,1,0:T(8,128)(2,1)S(1)}, u32[]{:S(2)}, u32[]{:S(2)}) async-start(bf16[32,64,128]{2,1,0:T(8,128)(2,1)} %get-tuple-element.29), calls=%async_computation.5 | async-start | bytes 1048576 | tf_op jit(solution)/shard_map/all_to_all | solution.py:217
